TPU v7x, 768 devices: a whole 4x8x12 slice. The times are simulated.
768 devices in a mesh: mem: 4 (over x), reg: 192 (over z, y, core).
Axes of the slice: x: 4, y: 8, z: 12, core: 2. Of those that a mesh axis runs over, the one named last changes fastest.
Arguments:
- members: bfloat16 [512, 6144, 128], P('mem', 'reg'), may hold values from -6 to 6
- diffusivity: float32 [6144, 128], P('reg'), may hold values from 0.02 to 0.2
- advection: float32 [6144, 128], P('reg'), may hold values from -0.3 to 0.3
- obs_value: bfloat16 [192, 4, 256], P('reg', 'mem'), may hold values from -6 to 6
- obs_rinv: float32 [192, 4, 256], P('reg', 'mem'), may hold values from 0.5 to 4
- obs_cell: int32 [192, 4, 256], P('reg', 'mem'), may hold values from 0 to 1023
- obs_count: int32 [192, 4], P('reg', 'mem'), may hold values from 64 to 256, as said below
- loc_index: int32 [192, 4, 256], P('reg', 'mem'), may hold values from 0 to 7
Outputs:
- analysis: float32 [512, 6144, 128], P('mem', 'reg')
Inputs may be any that keep to these rules, and one draw needn't show every extreme that they name: `obs_count`: each patch has 64 to 256 live slots, and some patch has exactly 256.
All inputs are finite; a program needn't handle non-finite values.
Results may differ from a plain program's by a relative error of at most 0.0047.
Values may be sent and summed in bfloat16 or wider, within the bound.
No kernel may reach another device: no remote copies, remote signals or barrier semaphores. Data moves between devices by JAX's collectives and lax.ppermute only.
A program may use at most 32 MiB of HBM per device.

v0:
```python
import jax
import jax.numpy as jnp
from jax import lax
from jax.sharding import PartitionSpec as P

STEPS = 3
NSIT = 2


def with_halo(cells, sides, width):
    for axis, dim in sides:
        count = lax.axis_size(axis)
        head = lax.slice_in_dim(cells, 0, width, axis=dim)
        tail = lax.slice_in_dim(cells, cells.shape[dim] - width, cells.shape[dim], axis=dim)
        cells = jnp.concatenate(
            [
                lax.ppermute(tail, axis, [(i, (i + 1) % count) for i in range(count)]),
                cells,
                lax.ppermute(head, axis, [((i + 1) % count, i) for i in range(count)]),
            ],
            axis=dim,
        )
    return cells


def advance(padded, diffusion, advect):
    centre = padded[:, 1:-1]
    north_row = padded[:, :-2]
    south_row = padded[:, 2:]
    east_cell = jnp.roll(centre, -1, 2)
    west_cell = jnp.roll(centre, 1, 2)
    return (
        centre
        + diffusion * (north_row + south_row + east_cell + west_cell - 4.0 * centre)
        - advect * 0.5 * (south_row - north_row)
    )


def analyse(states, ens_obs, value_all, prec_all):
    members_count = states.shape[0]
    identity = jnp.eye(members_count, dtype=jnp.float32)
    obs_float = ens_obs.astype(jnp.float32)
    obs_mean = jnp.mean(obs_float, axis=0)
    obs_perturb = obs_float - obs_mean[None, :]
    innovation = value_all - obs_mean
    weighted = obs_perturb * prec_all[None, :]
    system = (
        jnp.dot(weighted, obs_perturb.T, precision=lax.Precision.HIGHEST)
        + (members_count - 1.0) * identity
    )
    forcing = jnp.dot(weighted, innovation, precision=lax.Precision.HIGHEST)
    scale_value = jnp.sqrt(jnp.sum(system * system))
    root_iter = system / scale_value
    inverse_root = identity
    for sweep in range(NSIT):
        correction = 1.5 * identity - 0.5 * jnp.dot(
            inverse_root, root_iter, precision=lax.Precision.HIGHEST
        )
        root_iter = jnp.dot(root_iter, correction, precision=lax.Precision.HIGHEST)
        inverse_root = jnp.dot(correction, inverse_root, precision=lax.Precision.HIGHEST)
    mean_weights = (
        jnp.dot(
            inverse_root,
            jnp.dot(inverse_root, forcing, precision=lax.Precision.HIGHEST),
            precision=lax.Precision.HIGHEST,
        )
        / scale_value
    )
    transform = (
        jnp.sqrt((members_count - 1.0) / scale_value) * inverse_root + mean_weights[:, None]
    ).astype(jnp.bfloat16)
    state_float = states.astype(jnp.float32)
    state_mean = jnp.mean(state_float, axis=0)
    state_perturb = (state_float - state_mean[None, :]).astype(jnp.bfloat16)
    return state_mean[None, :] + jnp.dot(
        transform.T, state_perturb, preferred_element_type=jnp.float32
    )


def on_device(members, diffusivity, advection, obs_value, obs_rinv, obs_cell, obs_count, loc_index):
    ensemble_sample_array = members.astype(jnp.float32)
    padded = with_halo(ensemble_sample_array.astype(jnp.bfloat16), (("reg", 1),), STEPS).astype(
        ensemble_sample_array.dtype
    )
    coefficients = with_halo(jnp.stack([diffusivity, advection]), (("reg", 1),), STEPS)
    total_rows = coefficients.shape[1]
    for level_index in range(STEPS):
        inner_rows = coefficients[:, level_index + 1 : total_rows - level_index - 1]
        padded = advance(padded, inner_rows[0], inner_rows[1])
    ensemble_sample_array = padded
    propagate_ensemble = ensemble_sample_array.astype(jnp.bfloat16)
    zone_ensemble, lines_in_zone, lattice_breadth = propagate_ensemble.shape
    grouped_members = lax.axis_size("mem")
    rows_per_patch = lines_in_zone // grouped_members
    refolded_values = propagate_ensemble.reshape(
        zone_ensemble, grouped_members, rows_per_patch * lattice_breadth
    )
    owned = lax.all_to_all(refolded_values, "mem", split_axis=1, concat_axis=0, tiled=True)
    states = owned[:, 0]
    obs_cells = obs_cell[0, 0]
    obs_space = jnp.take(states, obs_cells, axis=1)
    slot_index = jnp.arange(obs_cells.shape[0], dtype=jnp.int32)
    live_slot = (slot_index < obs_count[0, 0]).astype(jnp.float32)
    own_prec = obs_rinv[0, 0] * live_slot
    loc_float = loc_index[0, 0].astype(jnp.float32)
    far_prec = (own_prec * jnp.exp(-(((loc_float + 1.0) / 4.0) ** 2))).astype(jnp.bfloat16)
    obs_info = jnp.stack([obs_value[0, 0], far_prec])
    space_pad, info_pad = (
        with_halo(obs_space[None], (("reg", 0),), 1),
        with_halo(obs_info[None], (("reg", 0),), 1),
    )
    ens_obs = jnp.concatenate([obs_space, space_pad[0], space_pad[2]], axis=1)
    value_all = jnp.concatenate([obs_value[0, 0], info_pad[0, 0], info_pad[2, 0]]).astype(
        jnp.float32
    )
    prec_all = jnp.concatenate(
        [own_prec, info_pad[0, 1].astype(jnp.float32), info_pad[2, 1].astype(jnp.float32)]
    )
    analysed = analyse(states, ens_obs, value_all, prec_all)
    shaped_back = analysed.reshape(analysed.shape[0], rows_per_patch, lattice_breadth)
    returned = lax.all_to_all(shaped_back, "mem", split_axis=0, concat_axis=1, tiled=True)
    return returned


def solution(mesh):
    return jax.shard_map(
        on_device,
        mesh=mesh,
        in_specs=(
            P("mem", "reg", None),
            P("reg", None),
            P("reg", None),
            P("reg", "mem", None),
            P("reg", "mem", None),
            P("reg", "mem", None),
            P("reg", "mem"),
            P("reg", "mem", None),
        ),
        out_specs=P("mem", "reg", None),
        check_vma=False,
    )
```

profile of v0, /device:TPU:2, one launch (start us, length us, event | category | flops | bytes accessed | tf_op | source)
XLA Modules:
  0.0 130.1 jit_solution(13370233284359922978)
XLA Ops:
  0.7 0.7 fusion.38
  1.4 0.7 maximum_bitcast_fusion
  2.1 1.9 %collective-permute-start.6 = (bf16[1,2,256]{2,1,0:T(2,128)(2,1)S(1)}, bf16[1,2,256]{2,1,0:T(2,128)(2,1)S(1)}, u32[]{:S(2)}, u32[]{:S(2)}) collective-permute-start(bf16[1,2,256]{2,1,0:T(2,128)(2,1)S(1)} %maximum_bitcast_fusion), channel_id=1, source_target_pairs={{0,1},{1,2},{2,3},{3,4},{4,5},{5,6},{6,7},{7,8},{8,9},{9,10},{10,1... | collective-permute-start | bytes 3080 | tf_op jit(solution)/shard_map/ppermute | solution.py:17
  4.0 16.9 %collective-permute-start.7 = (bf16[1,2,256]{2,1,0:T(2,128)(2,1)S(1)}, bf16[1,2,256]{2,1,0:T(2,128)(2,1)S(1)}, u32[]{:S(2)}, u32[]{:S(2)}) collective-permute-start(bf16[1,2,256]{2,1,0:T(2,128)(2,1)S(1)} %maximum_bitcast_fusion), channel_id=1, source_target_pairs={{1,0},{2,1},{3,2},{4,3},{5,4},{6,5},{7,6},{8,7},{9,8},{10,9},{11,1... | collective-permute-start | bytes 3080 | tf_op jit(solution)/shard_map/ppermute | solution.py:19
  20.9 0.7 pad_maximum_fusion.3
  21.7 1.9 %collective-permute-start.2 = (f32[2,3,128]{2,1,0:T(4,128)S(1)}, f32[2,3,128]{2,1,0:T(4,128)S(1)}, u32[]{:S(2)}, u32[]{:S(2)}) collective-permute-start(f32[2,3,128]{2,1,0:T(4,128)S(1)} %get-tuple-element.23), channel_id=1, source_target_pairs={{0,1},{1,2},{2,3},{3,4},{4,5},{5,6},{6,7},{7,8},{8,9},{9,10},{10,1... | collective-permute-start | bytes 9224 | tf_op jit(solution)/shard_map/ppermute | solution.py:17
  23.6 7.0 %collective-permute-start.3 = (f32[2,3,128]{2,1,0:T(4,128)S(1)}, f32[2,3,128]{2,1,0:T(4,128)S(1)}, u32[]{:S(2)}, u32[]{:S(2)}) collective-permute-start(f32[2,3,128]{2,1,0:T(4,128)S(1)} %get-tuple-element.24), channel_id=1, source_target_pairs={{1,0},{2,1},{3,2},{4,3},{5,4},{6,5},{7,6},{8,7},{9,8},{10,9},{11,1... | collective-permute-start | bytes 9224 | tf_op jit(solution)/shard_map/ppermute | solution.py:19
  30.5 1.1 fusion.45
  31.7 1.9 %collective-permute-start = (bf16[128,3,128]{2,1,0:T(4,128)(2,1)S(1)}, bf16[128,3,128]{2,1,0:T(4,128)(2,1)S(1)}, u32[]{:S(2)}, u32[]{:S(2)}) collective-permute-start(bf16[128,3,128]{2,1,0:T(4,128)(2,1)S(1)} %get-tuple-element.17), channel_id=1, source_target_pairs={{0,1},{1,2},{2,3},{3,4},{4,5},{5,6},{6,7},{7,8},{8,9},{9,10},{10,1... | collective-permute-start | bytes 294920 | tf_op jit(solution)/shard_map/ppermute | solution.py:17
  33.6 0.7 broadcast_multiply_fusion
  34.3 0.7 compare_select_fusion
  35.0 0.7 compare_select_fusion.3
  35.7 7.0 %collective-permute-start.1 = (bf16[128,3,128]{2,1,0:T(4,128)(2,1)S(1)}, bf16[128,3,128]{2,1,0:T(4,128)(2,1)S(1)}, u32[]{:S(2)}, u32[]{:S(2)}) collective-permute-start(bf16[128,3,128]{2,1,0:T(4,128)(2,1)S(1)} %get-tuple-element.18), channel_id=1, source_target_pairs={{1,0},{2,1},{3,2},{4,3},{5,4},{6,5},{7,6},{8,7},{9,8},{10,9},{11,1... | collective-permute-start | bytes 294920 | tf_op jit(solution)/shard_map/ppermute | solution.py:19
  42.7 0.7 pad_maximum_fusion.1
  43.5 1.7 %collective-permute-done.1 = bf16[128,3,128]{2,1,0:T(4,128)(2,1)S(1)} collective-permute-done((bf16[128,3,128]{2,1,0:T(4,128)(2,1)S(1)}, bf16[128,3,128]{2,1,0:T(4,128)(2,1)S(1)}, u32[]{:S(2)}, u32[]{:S(2)}) %collective-permute-start.1) | collective-permute-done | bytes 98336 | tf_op jit(solution)/shard_map/ppermute | solution.py:19
  45.2 1.8 %maximum_convert_fusion = f32[128,38,128]{2,1,0:T(8,128)S(1)} fusion(bf16[128,3,128]{2,1,0:T(4,128)(2,1)S(1)} %collective-permute-done.1, bf16[128,32,128]{2,1,0:T(8,128)(2,1)} %param.8, bf16[128,3,128]{2,1,0:T(4,128)(2,1)S(1)} %collective-permute-done), kind=kLoop, calls=%fused_computation.35 | loop fusion | flops 3735552 | bytes 3735552 | tf_op jit(solution)/shard_map/convert_element_type | solution.py:82
  47.0 0.9 fusion.43
  48.0 0.9 fusion.44
  48.9 2.2 %fusion.4 = f32[128,36,128]{2,1,0:T(8,128)S(1)} fusion(f32[128,36,1]{2,1,0:T(8,128)S(1)} %get-tuple-element.14, f32[128,36,127]{2,1,0:T(8,128)S(1)} %get-tuple-element.16, f32[128,36,127]{2,1,0:T(8,128)S(1)} %get-tuple-element.15, f32[128,36,1]{2,1,0:T(8,128)S(1)} %get-tuple-element.13, f32[128,38,128]{2,1,0:T(8,128)S(1)} %maximum_convert_fusion, ...), kind=kLoop, calls=%fused_computation.6 | loop fusion | flops 7077888 | bytes 14192640 | tf_op jit(solution)/shard_map/sub | solution.py:33
  51.1 0.9 fusion.41
  52.0 0.9 fusion.42
  53.0 2.2 %fusion.9 = f32[128,34,128]{2,1,0:T(8,128)S(1)} fusion(f32[128,34,1]{2,1,0:T(8,128)S(1)} %get-tuple-element.10, f32[128,34,127]{2,1,0:T(8,128)S(1)} %get-tuple-element.12, f32[128,34,127]{2,1,0:T(8,128)S(1)} %get-tuple-element.11, f32[128,34,1]{2,1,0:T(8,128)S(1)} %get-tuple-element.9, f32[128,36,128]{2,1,0:T(8,128)S(1)} %fusion.4, ...), kind=kLoop, calls=%fused_computation.12 | loop fusion | flops 6684672 | bytes 13404160 | tf_op jit(solution)/shard_map/sub | solution.py:33
  55.1 0.9 fusion.39
  56.0 0.9 fusion.40
  56.9 1.7 %fusion.19 = bf16[128,32,128]{2,1,0:T(8,128)(2,1)S(1)} fusion(f32[128,32,1]{2,1,0:T(8,128)S(1)} %get-tuple-element.6, f32[128,32,127]{2,1,0:T(8,128)S(1)} %get-tuple-element.8, f32[128,32,127]{2,1,0:T(8,128)S(1)} %get-tuple-element.7, f32[128,32,1]{2,1,0:T(8,128)S(1)} %get-tuple-element.5, f32[128,34,128]{2,1,0:T(8,128)S(1)} %fusion.9, ...), kind=kLoop, calls=%fused_computation.23 | loop fusion | flops 6815744 | bytes 11567104 | tf_op jit(solution)/shard_map/convert_element_type | solution.py:91
  58.6 0.3 reshape.136
  58.9 1.3 copy.12
  60.2 4.8 %all-to-all-start = ((bf16[128,4,1024]{2,0,1:T(8,128)(2,1)}), bf16[128,4,1024]{2,0,1:T(8,128)(2,1)S(1)}, u32[]{:S(2)}, u32[]{:S(2)}) async-start(bf16[128,4,1024]{2,0,1:T(8,128)(2,1)} %copy.12), calls=%async_computation | async-start | bytes 2097152 | tf_op jit(solution)/shard_map/all_to_all | solution.py:98
  65.1 9.3 %all-to-all-done = bf16[128,4,1024]{2,0,1:T(8,128)(2,1)S(1)} async-done(((bf16[128,4,1024]{2,0,1:T(8,128)(2,1)}), bf16[128,4,1024]{2,0,1:T(8,128)(2,1)S(1)}, u32[]{:S(2)}, u32[]{:S(2)}) %all-to-all-start) | async-done | bytes 1048608 | tf_op jit(solution)/shard_map/all_to_all | solution.py:98
  74.4 0.5 copy.13
  75.0 1.2 gather_fusion
  76.2 1.9 %collective-permute-start.4 = (bf16[1,512,256]{1,2,0:T(8,128)(2,1)S(1)}, bf16[1,512,256]{1,2,0:T(8,128)(2,1)S(1)}, u32[]{:S(2)}, u32[]{:S(2)}) collective-permute-start(bf16[1,512,256]{1,2,0:T(8,128)(2,1)S(1)} %bitcast_select_fusion), channel_id=1, source_target_pairs={{0,1},{1,2},{2,3},{3,4},{4,5},{5,6},{6,7},{7,8},{8,9},{9,10},{10,1... | collective-permute-start | bytes 786440 | tf_op jit(solution)/shard_map/ppermute | solution.py:17
  78.2 7.1 %collective-permute-start.5 = (bf16[1,512,256]{1,2,0:T(8,128)(2,1)S(1)}, bf16[1,512,256]{1,2,0:T(8,128)(2,1)S(1)}, u32[]{:S(2)}, u32[]{:S(2)}) collective-permute-start(bf16[1,512,256]{1,2,0:T(8,128)(2,1)S(1)} %bitcast_select_fusion), channel_id=1, source_target_pairs={{1,0},{2,1},{3,2},{4,3},{5,4},{6,5},{7,6},{8,7},{9,8},{10,9},{11,1... | collective-permute-start | bytes 786440 | tf_op jit(solution)/shard_map/ppermute | solution.py:19
  85.6 1.6 %collective-permute-done.4 = bf16[1,512,256]{1,2,0:T(8,128)(2,1)S(1)} collective-permute-done((bf16[1,512,256]{1,2,0:T(8,128)(2,1)S(1)}, bf16[1,512,256]{1,2,0:T(8,128)(2,1)S(1)}, u32[]{:S(2)}, u32[]{:S(2)}) %collective-permute-start.4) | collective-permute-done | bytes 262176 | tf_op jit(solution)/shard_map/ppermute | solution.py:17
  87.3 1.8 %collective-permute-done.5 = bf16[1,512,256]{1,2,0:T(8,128)(2,1)S(1)} collective-permute-done((bf16[1,512,256]{1,2,0:T(8,128)(2,1)S(1)}, bf16[1,512,256]{1,2,0:T(8,128)(2,1)S(1)}, u32[]{:S(2)}, u32[]{:S(2)}) %collective-permute-start.5) | collective-permute-done | bytes 262176 | tf_op jit(solution)/shard_map/ppermute | solution.py:19
  89.2 4.1 %multiply_reduce_fusion = (f32[]{:T(128)}, f32[512,512]{1,0:T(8,128)S(1)}) fusion(f32[768]{0:T(1024)S(1)} %get-tuple-element.26, bf16[512,256]{0,1:T(8,128)(2,1)S(1)} %bitcast.79, bf16[512,256]{0,1:T(8,128)(2,1)S(1)} %bitcast.76, bf16[512,256]{0,1:T(8,128)(2,1)S(1)} %bitcast_select_fusion.1, f32[768]{0:T(1024)S(1)} %pad_maximum_fusion.4), kind=kOutput, calls=%fused_computation.39 | convolution fusion | flops 2423128064 | bytes 1841156 | tf_op jit(solution)/shard_map/dot_general | solution.py:48
  94.0 1.1 select_subtract_fusion.1
  95.1 1.9 %fusion.34 = f32[512,512]{1,0:T(8,128)S(1)} fusion(f32[512,512]{1,0:T(8,128)S(1)} %select_subtract_fusion.1, f32[512,512]{1,0:T(8,128)S(1)} %get-tuple-element.32, f32[]{:T(128)S(6)} %sqrt.6), kind=kOutput, calls=%fused_computation.51 | convolution fusion | flops 1610874880 | bytes 3145732 | tf_op jit(solution)/shard_map/dot_general | solution.py:59
  97.0 1.0 fusion.26
  98.0 1.1 fusion.23
  99.1 1.9 %select_subtract_fusion = f32[512,512]{1,0:T(8,128)S(1)} fusion(f32[512,512]{1,0:T(8,128)S(1)} %fusion.26, f32[512,512]{1,0:T(8,128)S(1)} %fusion.34), kind=kOutput, calls=%fused_computation.30 | convolution fusion | flops 1611661312 | bytes 3145728 | tf_op jit(solution)/shard_map/dot_general | solution.py:56
  101.0 2.1 %fusion.46 = f32[512,512]{1,0:T(8,128)S(1)} fusion(f32[512,512]{1,0:T(8,128)S(1)} %select_subtract_fusion, f32[512,512]{1,0:T(8,128)S(1)} %fusion.26), kind=kOutput, calls=%fused_computation.89 | convolution fusion | flops 1610612736 | bytes 3145728 | tf_op jit(solution)/shard_map/dot_general | solution.py:60
  103.1 1.0 convolution_bitcast_fusion
  104.0 1.0 fusion.47
  105.2 0.8 add_bitcast_fusion
  106.0 0.5 copy.15
  106.5 22.0 %all_to_all.33 = f32[512,8,128]{2,1,0:T(8,128)S(1)} all-to-all(f32[512,8,128]{2,1,0:T(8,128)S(1)} %bitcast.73), channel_id=1, replica_groups=mesh['mem'=4,'reg'=192] {'mem'}, dimensions={0} | all-to-all | bytes 4194304 | tf_op jit(solution)/shard_map/all_to_all | solution.py:121
  128.4 1.6 %copy.17 = f32[4,128,8,128]{3,2,0,1:T(8,128)} copy(f32[4,128,8,128]{3,2,1,0:T(8,128)S(1)} %bitcast.74) | data formatting | bytes 4194304 | tf_op jit(solution)/shard_map/all_to_all | solution.py:121
  (27 shorter events, 0.7 us)
Async XLA Ops:
  2.1 63.0 %collective-permute-start.6 = (bf16[1,2,256]{2,1,0:T(2,128)(2,1)S(1)}, bf16[1,2,256]{2,1,0:T(2,128)(2,1)S(1)}, u32[]{:S(2)}, u32[]{:S(2)}) collective-permute-start(bf16[1,2,256]{2,1,0:T(2,128)(2,1)S(1)} %maximum_bitcast_fusion), channel_id=1, source_target_pairs={{0,1},{1,2},{2,3},{3,4},{4,5},{5,6},{6,7},{7,8},{8,9},{9,10},{10,1... | collective-permute-start | bytes 3080 | tf_op jit(solution)/shard_map/ppermute | solution.py:17
  4.0 61.1 %collective-permute-start.7 = (bf16[1,2,256]{2,1,0:T(2,128)(2,1)S(1)}, bf16[1,2,256]{2,1,0:T(2,128)(2,1)S(1)}, u32[]{:S(2)}, u32[]{:S(2)}) collective-permute-start(bf16[1,2,256]{2,1,0:T(2,128)(2,1)S(1)} %maximum_bitcast_fusion), channel_id=1, source_target_pairs={{1,0},{2,1},{3,2},{4,3},{5,4},{6,5},{7,6},{8,7},{9,8},{10,9},{11,1... | collective-permute-start | bytes 3080 | tf_op jit(solution)/shard_map/ppermute | solution.py:19
  21.7 14.1 %collective-permute-start.2 = (f32[2,3,128]{2,1,0:T(4,128)S(1)}, f32[2,3,128]{2,1,0:T(4,128)S(1)}, u32[]{:S(2)}, u32[]{:S(2)}) collective-permute-start(f32[2,3,128]{2,1,0:T(4,128)S(1)} %get-tuple-element.23), channel_id=1, source_target_pairs={{0,1},{1,2},{2,3},{3,4},{4,5},{5,6},{6,7},{7,8},{8,9},{9,10},{10,1... | collective-permute-start | bytes 9224 | tf_op jit(solution)/shard_map/ppermute | solution.py:17
  23.6 19.1 %collective-permute-start.3 = (f32[2,3,128]{2,1,0:T(4,128)S(1)}, f32[2,3,128]{2,1,0:T(4,128)S(1)}, u32[]{:S(2)}, u32[]{:S(2)}) collective-permute-start(f32[2,3,128]{2,1,0:T(4,128)S(1)} %get-tuple-element.24), channel_id=1, source_target_pairs={{1,0},{2,1},{3,2},{4,3},{5,4},{6,5},{7,6},{8,7},{9,8},{10,9},{11,1... | collective-permute-start | bytes 9224 | tf_op jit(solution)/shard_map/ppermute | solution.py:19
  31.7 11.8 %collective-permute-start = (bf16[128,3,128]{2,1,0:T(4,128)(2,1)S(1)}, bf16[128,3,128]{2,1,0:T(4,128)(2,1)S(1)}, u32[]{:S(2)}, u32[]{:S(2)}) collective-permute-start(bf16[128,3,128]{2,1,0:T(4,128)(2,1)S(1)} %get-tuple-element.17), channel_id=1, source_target_pairs={{0,1},{1,2},{2,3},{3,4},{4,5},{5,6},{6,7},{7,8},{8,9},{9,10},{10,1... | collective-permute-start | bytes 294920 | tf_op jit(solution)/shard_map/ppermute | solution.py:17
  35.7 9.5 %collective-permute-start.1 = (bf16[128,3,128]{2,1,0:T(4,128)(2,1)S(1)}, bf16[128,3,128]{2,1,0:T(4,128)(2,1)S(1)}, u32[]{:S(2)}, u32[]{:S(2)}) collective-permute-start(bf16[128,3,128]{2,1,0:T(4,128)(2,1)S(1)} %get-tuple-element.18), channel_id=1, source_target_pairs={{1,0},{2,1},{3,2},{4,3},{5,4},{6,5},{7,6},{8,7},{9,8},{10,9},{11,1... | collective-permute-start | bytes 294920 | tf_op jit(solution)/shard_map/ppermute | solution.py:19
  56.0 0.9 copy-start
  58.9 6.1 %copy-start.2 = (s32[1,1,256]{2,1,0:T(1,128)S(1)}, s32[1,1,256]{2,1,0:T(1,128)}, u32[]{:S(2)}) copy-start(s32[1,1,256]{2,1,0:T(1,128)} %param.13) | copy-start | bytes 3076
  58.9 6.1 %copy-start.1 = (bf16[1,1,256]{2,1,0:T(2,128)(2,1)S(1)}, bf16[1,1,256]{2,1,0:T(2,128)(2,1)}, u32[]{:S(2)}) copy-start(bf16[1,1,256]{2,1,0:T(2,128)(2,1)} %param.11) | copy-start | bytes 1540
  60.2 14.3 %all-to-all-start = ((bf16[128,4,1024]{2,0,1:T(8,128)(2,1)}), bf16[128,4,1024]{2,0,1:T(8,128)(2,1)S(1)}, u32[]{:S(2)}, u32[]{:S(2)}) async-start(bf16[128,4,1024]{2,0,1:T(8,128)(2,1)} %copy.12), calls=%async_computation | async-start | bytes 2097152 | tf_op jit(solution)/shard_map/all_to_all | solution.py:98
  76.2 11.0 %collective-permute-start.4 = (bf16[1,512,256]{1,2,0:T(8,128)(2,1)S(1)}, bf16[1,512,256]{1,2,0:T(8,128)(2,1)S(1)}, u32[]{:S(2)}, u32[]{:S(2)}) collective-permute-start(bf16[1,512,256]{1,2,0:T(8,128)(2,1)S(1)} %bitcast_select_fusion), channel_id=1, source_target_pairs={{0,1},{1,2},{2,3},{3,4},{4,5},{5,6},{6,7},{7,8},{8,9},{9,10},{10,1... | collective-permute-start | bytes 786440 | tf_op jit(solution)/shard_map/ppermute | solution.py:17
  78.2 10.8 %collective-permute-start.5 = (bf16[1,512,256]{1,2,0:T(8,128)(2,1)S(1)}, bf16[1,512,256]{1,2,0:T(8,128)(2,1)S(1)}, u32[]{:S(2)}, u32[]{:S(2)}) collective-permute-start(bf16[1,512,256]{1,2,0:T(8,128)(2,1)S(1)} %bitcast_select_fusion), channel_id=1, source_target_pairs={{1,0},{2,1},{3,2},{4,3},{5,4},{6,5},{7,6},{8,7},{9,8},{10,9},{11,1... | collective-permute-start | bytes 786440 | tf_op jit(solution)/shard_map/ppermute | solution.py:19
where the time goes:
time: 131 us; the launch traced here: 130 us
  starting transfers between devices  50.5 us (39%)
  blocking collectives  22 us (17%)
  matrix products  15.9 us (12%)
  waiting for transfers between devices  14.4 us (11%)
  other arithmetic  13.5 us (10%)
  local copies, waits for them, and re-layouts  11.9 us (9%)
  between operations  1.81 us (1%)
    ppermute x4, starting transfers between devices, with_halo(): lax.ppermute(head, axis, [((i + 1) % count, i) for i in range(count)])  38 us
    all_to_all x1, blocking collectives, on_device(): lax.all_to_all(shaped_back, 'mem', split_axis=0, concat_axis=1, tiled=True)  22 us
    all_to_all x1, waiting for transfers between devices, on_device(): lax.all_to_all(refolded_values, 'mem', split_axis=1, concat_axis=0, tiled...  9.31 us
    ppermute x4, starting transfers between devices, with_halo(): lax.ppermute(tail, axis, [(i, (i + 1) % count) for i in range(count)])  7.66 us
    slice x6, local copies, waits for them, and re-layouts, advance(): west_cell = jnp.roll(centre, 1, 2)  5.44 us
    all_to_all x1, starting transfers between devices, on_device(): lax.all_to_all(refolded_values, 'mem', split_axis=1, concat_axis=0, tiled...  4.82 us
    sub x2, other arithmetic, advance(): centre + diffusion * (north_row + south_row + east_cell + west_cell - 4.0...  4.36 us
    dot_general x1, matrix products, analyse(): jnp.dot(weighted, obs_perturb.T, precision=lax.Precision.HIGHEST)  4.06 us
  transfers between devices with their start and end apart: 9, of which 4 were waited for; matrix products, arithmetic and copies ran while one was open for 15% of the time, Pallas kernels for 0%

commit v1 on v0

v1 whole, which is shorter than its diff:
```python
import jax
import jax.numpy as jnp
from jax import lax
from jax.experimental import pallas as pl
from jax.experimental.pallas import tpu as pltpu
from jax.sharding import PartitionSpec as P

STEPS = 3
NSIT = 2
LANES = 128
BF = jnp.bfloat16
F32 = jnp.float32
VMEM = pl.BlockSpec(memory_space=pltpu.VMEM)
SMEM = pl.BlockSpec(memory_space=pltpu.SMEM)


def call(body, outs, n_in, scratch=(), specs=None, flops=0, moved=0, name=None):
    return pl.pallas_call(
        body,
        out_shape=[jax.ShapeDtypeStruct(s, d) for s, d in outs],
        in_specs=specs or [VMEM] * n_in,
        out_specs=[VMEM] * len(outs),
        scratch_shapes=list(scratch),
        cost_estimate=pl.CostEstimate(flops=flops, bytes_accessed=moved, transcendentals=0),
        compiler_params=pltpu.CompilerParams(vmem_limit_bytes=40 << 20),
        name=name,
    )


def pack_body(x_ref, d_ref, a_ref, sa_ref, sb_ref, rows, coef):
    members = x_ref.shape[0]
    lines = x_ref.shape[1]

    def edge(out_ref, tail):
        base = lines - 8 if tail else 0
        rows[...] = x_ref[:, base : base + 8, :].astype(F32).reshape(members * 8, LANES)
        first = 8 - STEPS if tail else 0
        for k in range(STEPS):
            out_ref[k * members : (k + 1) * members, :] = rows[
                pl.ds(first + k, members, stride=8), :
            ].astype(BF)
        at = lines - 2 if tail else 0
        coef[0:2, :] = d_ref[at : at + 2, :]
        coef[2:4, :] = a_ref[at : at + 2, :]
        whole = coef[0:4, :]
        high = whole.astype(BF).astype(F32)
        middle = (whole - high).astype(BF).astype(F32)
        coef[0:4, :] = high
        coef[4:8, :] = middle
        coef[8:12, :] = whole - high - middle
        coef[12:16, :] = jnp.zeros((4, LANES), F32)
        out_ref[STEPS * members :, :] = coef[...].astype(BF)

    even = lax.rem(lax.axis_index("reg"), 2) == 0

    @pl.when(even)
    def _():
        edge(sa_ref, True)
        edge(sb_ref, False)

    @pl.when(jnp.logical_not(even))
    def _():
        edge(sa_ref, False)
        edge(sb_ref, True)


def forecast_body(x_ref, ra_ref, rb_ref, d_ref, a_ref, o_ref, xs, halo, dd, aa, cf):
    members = x_ref.shape[0]
    lines = x_ref.shape[1]
    reach = STEPS * members
    even = lax.rem(lax.axis_index("reg"), 2) == 0

    def take(ref, side):
        halo[side * reach : (side + 1) * reach, :] = ref[0:reach, :].astype(F32)
        parts = ref[reach:, :].astype(F32)
        whole = parts[0:4] + parts[4:8] + parts[8:12]
        at = (lines + 2) if side else 0
        dd[at : at + 2, :] = whole[0:2]
        aa[at : at + 2, :] = whole[2:4]

    @pl.when(even)
    def _():
        take(rb_ref, 0)
        take(ra_ref, 1)

    @pl.when(jnp.logical_not(even))
    def _():
        take(ra_ref, 0)
        take(rb_ref, 1)

    dd[2 : 2 + lines, :] = d_ref[...]
    aa[2 : 2 + lines, :] = a_ref[...]
    for row in range(lines + 4):
        dif = jnp.broadcast_to(dd[row : row + 1, :], (8, LANES))
        adv = 0.5 * jnp.broadcast_to(aa[row : row + 1, :], (8, LANES))
        cf[row, 0:8, :] = 1.0 - 4.0 * dif
        cf[row, 8:16, :] = dif
        cf[row, 16:24, :] = dif + adv
        cf[row, 24:32, :] = dif - adv

    block = 16

    def step(b, carry):
        xs[...] = x_ref[pl.ds(b * block, block)].astype(F32).reshape(block * lines, LANES)

        def start_row(row):
            if row < 0:
                return halo[pl.ds((row + STEPS) * members + b * block, block), :]
            if row >= lines:
                return halo[pl.ds(reach + (row - lines) * members + b * block, block), :]
            return xs[pl.ds(row, block, stride=lines), :]

        def update(row, north, centre, south):
            def c(k):
                v = cf[row + 2, 8 * k : 8 * k + 8, :]
                return jnp.concatenate([v, v], axis=0)

            sides = pltpu.roll(centre, 1, 1) + pltpu.roll(centre, LANES - 1, 1)
            return c(0) * centre + c(1) * sides + c(2) * north + c(3) * south

        levels = [{} for _ in range(STEPS + 1)]
        for row in range(-STEPS, lines + STEPS):
            levels[0][row] = start_row(row)
            for level in range(1, STEPS + 1):
                at = row - level
                prev = levels[level - 1]
                if at - 1 not in prev or at < level - STEPS:
                    continue
                new = update(at, prev[at - 1], prev[at], prev[at + 1])
                if level == STEPS:
                    o_ref[at, pl.ds(b * block, block), :] = new.astype(BF)
                else:
                    levels[level][at] = new
                del prev[at - 1]
        return carry

    lax.fori_loop(0, members // block, step, 0)


def observe_body(s_ref, cell_ref, value_ref, rinv_ref, count_ref, loc_ref, h_ref, prec_ref):
    groups, tile, per, _ = s_ref.shape
    members = groups * per
    slots = cell_ref.shape[-1]
    cell = cell_ref[0]
    total = jnp.zeros((members, slots), F32)
    line = lax.broadcasted_iota(jnp.int32, (2 * LANES, slots), 0)
    for pair in range(tile // 2):
        here = jnp.concatenate(
            [
                s_ref[:, 2 * pair].reshape(members, LANES),
                s_ref[:, 2 * pair + 1].reshape(members, LANES),
            ],
            axis=1,
        )
        picks = jnp.where(line + 2 * LANES * pair == cell, 1.0, 0.0).astype(BF)
        total += jnp.dot(here, picks, preferred_element_type=F32)
    h_ref[0:members, :] = total.astype(BF)
    slot = lax.broadcasted_iota(jnp.int32, (1, slots), 1)
    own = jnp.where(slot < count_ref[0, 0], rinv_ref[0], 0.0)
    radius = (loc_ref[0].astype(F32) + 1.0) / 4.0
    far = own * jnp.exp(-(radius * radius))
    row = lax.broadcasted_iota(jnp.int32, (16, slots), 0)
    value = value_ref[0].astype(F32)
    info = jnp.where(row == 0, value, jnp.where(row == 1, far, 0.0))
    h_ref[members:, :] = info.astype(BF)
    prec_ref[...] = jnp.where(
        lax.broadcasted_iota(jnp.int32, (8, slots), 0) == 0, own, value
    )


def weigh(obs, value, prec):
    count = obs.shape[0]
    mean = jnp.sum(obs, axis=0, keepdims=True) * (1.0 / count)
    perturb = obs - mean
    scaled = (perturb * jnp.sqrt(prec)).astype(BF)
    force = jnp.sum(perturb * (prec * (value - mean)), axis=1, keepdims=True)
    return scaled, force


def gram(a):
    return lax.dot_general(a, a, (((1,), (1,)), ((), ())), preferred_element_type=F32)


def own_body(s_ref, h_ref, prec_ref, xb_ref, xbar_ref, sys_ref, force_ref):
    groups, tile, per, _ = s_ref.shape
    members = groups * per
    for row in range(tile):
        here = s_ref[:, row].reshape(members, LANES).astype(F32)
        mean = jnp.sum(here, axis=0, keepdims=True) * (1.0 / members)
        xbar_ref[:, row * LANES : (row + 1) * LANES] = jnp.broadcast_to(mean, (8, LANES))
        xb_ref[:, row * LANES : (row + 1) * LANES] = (here - mean).astype(BF)
    scaled, force = weigh(h_ref[0:members, :].astype(F32), prec_ref[1:2, :], prec_ref[0:1, :])
    sys_ref[...] = gram(scaled)
    force_ref[...] = jnp.broadcast_to(force, (members, LANES))


def analyse_body(ra_ref, rb_ref, xb_ref, xbar_ref, sys_ref, force_ref, o_ref):
    members = sys_ref.shape[0]
    groups, tile, per, _ = o_ref.shape
    total = sys_ref[...]
    force = force_ref[:, 0:1]
    for ref in (ra_ref, rb_ref):
        info = ref[members:, :].astype(F32)
        scaled, more = weigh(ref[0:members, :].astype(F32), info[0:1, :], info[1:2, :])
        total += gram(scaled)
        force += more
    diagonal = lax.broadcasted_iota(jnp.int32, (members, members), 0) == lax.broadcasted_iota(
        jnp.int32, (members, members), 1
    )
    total += jnp.where(diagonal, members - 1.0, 0.0)
    inv = lax.rsqrt(jnp.sum(total * total))
    base = total * inv
    base_b = base.astype(BF)
    square = jnp.dot(base_b, base_b, preferred_element_type=F32)
    tail = (0.0625 * square - 0.5625 * base).astype(BF)
    root = (
        jnp.where(diagonal, 2.25, 0.0)
        - 2.4375 * base
        + 1.6875 * square
        + jnp.dot(square.astype(BF), tail, preferred_element_type=F32)
    )
    first = jnp.sum(root * force, axis=0, keepdims=True)
    second = jnp.sum(root * first, axis=1, keepdims=True) * inv
    mean_row = jnp.sum(jnp.where(diagonal, second, 0.0), axis=0, keepdims=True)
    weights = (jnp.sqrt((members - 1.0) * inv) * root + mean_row).astype(BF)
    for pair in range(tile // 2):
        cols = slice(2 * pair * LANES, 2 * (pair + 1) * LANES)
        new = xbar_ref[0:1, cols] + jnp.dot(
            weights, xb_ref[:, cols], preferred_element_type=F32
        )
        for half in range(2):
            part = new[:, half * LANES : (half + 1) * LANES].astype(BF)
            o_ref[:, 2 * pair + half] = part.reshape(groups, per, LANES)


def place_body(r_ref, o_ref, out):
    lines = r_ref.shape[0]
    block = o_ref.shape[0]
    b = pl.program_id(0)
    for row in range(lines):
        out[pl.ds(row, block, stride=lines), :] = r_ref[
            row, pl.ds(pl.multiple_of(b * block, block), block), :
        ].astype(F32)
    o_ref[...] = out[...].reshape(block, lines, LANES)


def on_device(members, diffusivity, advection, obs_value, obs_rinv, obs_cell, obs_count, loc_index):
    per, lines, _ = members.shape
    groups = lax.axis_size("mem")
    regions = lax.axis_size("reg")
    tile = lines // groups
    total = per * groups
    slots = obs_cell.shape[-1]
    near = [(i, i ^ 1) for i in range(regions)]
    across = [(i, (i + 1) % regions if i % 2 else (i - 1) % regions) for i in range(regions)]

    edge = ((STEPS * per + 16, LANES), BF)
    send_a, send_b = call(
        pack_body,
        [edge, edge],
        3,
        [pltpu.VMEM((per * 8, LANES), F32), pltpu.VMEM((16, LANES), F32)],
        moved=1 << 20,
        name="pack",
    )(members, diffusivity, advection)
    got_b = lax.ppermute(send_b, "reg", across)
    got_a = lax.ppermute(send_a, "reg", near)
    (ahead,) = call(
        forecast_body,
        [((lines, per, LANES), BF)],
        5,
        [
            pltpu.VMEM((16 * lines, LANES), F32),
            pltpu.VMEM((2 * STEPS * per, LANES), F32),
            pltpu.VMEM((lines + 8, LANES), F32),
            pltpu.VMEM((lines + 8, LANES), F32),
            pltpu.VMEM((lines + 4, 32, LANES), F32),
        ],
        moved=4 << 20,
        name="forecast",
    )(members, got_a, got_b, diffusivity, advection)
    states = lax.all_to_all(ahead.reshape(groups, tile, per, LANES), "mem", 0, 0)
    obs, prec = call(
        observe_body,
        [((total + 16, slots), BF), ((8, slots), F32)],
        6,
        specs=[VMEM, VMEM, VMEM, VMEM, SMEM, VMEM],
        flops=2 * total * tile * LANES * slots,
        moved=2 << 20,
        name="observe",
    )(states, obs_cell, obs_value, obs_rinv, obs_count, loc_index)
    nb = lax.ppermute(obs, "reg", across)
    na = lax.ppermute(obs, "reg", near)
    xb, xbar, system, force = call(
        own_body,
        [
            ((total, tile * LANES), BF),
            ((8, tile * LANES), F32),
            ((total, total), F32),
            ((total, LANES), F32),
        ],
        3,
        flops=2 * total * total * slots,
        moved=4 << 20,
        name="own",
    )(states, obs, prec)
    (back,) = call(
        analyse_body,
        [((groups, tile, per, LANES), BF)],
        6,
        flops=10 * total * total * total,
        moved=4 << 20,
        name="analyse",
    )(na, nb, xb, xbar, system, force)
    home = lax.all_to_all(back, "mem", 0, 0).reshape(lines, per, LANES)
    block = 32
    return pl.pallas_call(
        place_body,
        grid=(per // block,),
        out_shape=jax.ShapeDtypeStruct((per, lines, LANES), F32),
        in_specs=[VMEM],
        out_specs=pl.BlockSpec((block, lines, LANES), lambda i: (i, 0, 0)),
        scratch_shapes=[pltpu.VMEM((block * lines, LANES), F32)],
        compiler_params=pltpu.CompilerParams(vmem_limit_bytes=40 << 20),
        name="place",
    )(home)


def solution(mesh):
    return jax.shard_map(
        on_device,
        mesh=mesh,
        in_specs=(
            P("mem", "reg", None),
            P("reg", None),
            P("reg", None),
            P("reg", "mem", None),
            P("reg", "mem", None),
            P("reg", "mem", None),
            P("reg", "mem"),
            P("reg", "mem", None),
        ),
        out_specs=P("mem", "reg", None),
        check_vma=False,
    )
```

time: 131 us -> 83.9 us (0.64)
  Pallas kernels: 0 us -> 17.1 us
  matrix products: 15.9 us -> 0 us
  starting transfers between devices: 50.5 us -> 35 us
  other arithmetic: 13.5 us -> 0 us
  local copies, waits for them, and re-layouts: 11.9 us -> 2.68 us
  blocking collectives: 22 us -> 13.5 us
    pallas_call x0 -> x6, Pallas kernels: none -> 17.1 us  [the longest x1 9.86 us: on_device(): call(forecast_body, [((lines, per, LANES), BF)], 5, [pltpu.VMEM((16 * lin...]
    dot_general x10 -> x0, matrix products: 15.9 us -> none  [the longest x1 4.06 us: analyse(): jnp.dot(weighted, obs_perturb.T, precision=lax.Precision.HIGHEST)]
    ppermute x8 -> x4, starting transfers between devices: 45.6 us -> 30.1 us  [the longest x1 17.7 us: on_device(): got_b = lax.ppermute(send_b, 'reg', across)]
    all_to_all x1, blocking collectives: 22 us -> 13.5 us  [on_device(): home = lax.all_to_all(back, 'mem', 0, 0).reshape(lines, per, LANES)]
    slice x7 -> x0, local copies, waits for them, and re-layouts: 6.58 us -> none  [the longest x6 5.44 us: advance(): west_cell = jnp.roll(centre, 1, 2)]
    sub x3 -> x0, other arithmetic: 4.37 us -> none  [the longest x2 4.36 us: advance(): centre + diffusion * (north_row + south_row + east_cell + west_cell - 4.0...]
    convert_element_type x3 -> x0, other arithmetic: 4.23 us -> none  [the longest x1 1.85 us: on_device(): with_halo(ensemble_sample_array.astype(jnp.bfloat16), (('reg', 1),), STEPS)]
    unnamed x7 -> x14, local copies, waits for them, and re-layouts: 0.49 us -> 2.68 us
  transfers between devices with their start and end apart: 9 -> 5, of which waited for: 4 -> 3; matrix products, arithmetic and copies ran while one was open for 15% -> 0% of each run, Pallas kernels for 0% -> 1%
where the time goes in v1:
time: 83.9 us; the launch traced here: 83.5 us
  starting transfers between devices  35 us (42%)
  Pallas kernels  17.1 us (20%)
  waiting for transfers between devices  14.4 us (17%)
  blocking collectives  13.5 us (16%)
  local copies, waits for them, and re-layouts  2.68 us (3%)
    ppermute x1, starting transfers between devices, on_device(): got_b = lax.ppermute(send_b, 'reg', across)  17.7 us
    all_to_all x1, blocking collectives, on_device(): home = lax.all_to_all(back, 'mem', 0, 0).reshape(lines, per, LANES)  13.5 us
    pallas_call x1, Pallas kernels, on_device(): call(forecast_body, [((lines, per, LANES), BF)], 5, [pltpu.VMEM((16 * lin...  9.86 us
    all_to_all x1, waiting for transfers between devices, on_device(): lax.all_to_all(ahead.reshape(groups, tile, per, LANES), 'mem', 0, 0)  8.78 us
    ppermute x1, starting transfers between devices, on_device(): nb = lax.ppermute(obs, 'reg', across)  8.58 us
    all_to_all x1, starting transfers between devices, on_device(): lax.all_to_all(ahead.reshape(groups, tile, per, LANES), 'mem', 0, 0)  4.82 us
    ppermute x1, waiting for transfers between devices, on_device(): nb = lax.ppermute(obs, 'reg', across)  3.3 us
    pallas_call x1, Pallas kernels, on_device(): pl.pallas_call(place_body, grid=(per // block,), out_shape=jax.ShapeDtype...  3.18 us
  transfers between devices with their start and end apart: 5, of which 3 were waited for; matrix products, arithmetic and copies ran while one was open for 0% of the time, Pallas kernels for 1%

profile of v1, /device:TPU:2, one launch (start us, length us, event | category | flops | bytes accessed | tf_op | source)
XLA Modules:
  0.0 83.5 jit_solution(11982039133857095429)
XLA Ops:
  0.0 0.0 copy-start
  0.0 1.2 %copy-done = bf16[128,32,128]{2,1,0:T(8,128)(2,1)S(1)} copy-done((bf16[128,32,128]{2,1,0:T(8,128)(2,1)S(1)}, bf16[128,32,128]{2,1,0:T(8,128)(2,1)}, u32[]{:S(2)}) %copy-start) | copy-done | bytes 1048600
  1.2 0.0 copy-start.1
  1.2 0.7 copy-done.1
  1.9 0.0 copy-start.2
  1.9 0.7 copy-done.2
  2.7 0.1 pack.1
  2.8 1.9 %collective-permute-start = (bf16[400,128]{1,0:T(8,128)(2,1)S(1)}, bf16[400,128]{1,0:T(8,128)(2,1)S(1)}, u32[]{:S(2)}, u32[]{:S(2)}) collective-permute-start(bf16[400,128]{1,0:T(8,128)(2,1)S(1)} %get-tuple-element.13), channel_id=1, source_target_pairs={{0,1},{1,0},{2,3},{3,2},{4,5},{5,4},{6,7},{7,6},{8,9},{9,8},{10,11... | collective-permute-start | bytes 307208 | tf_op jit(solution)/shard_map/ppermute | solution.py:267
  4.7 0.0 copy-start.3
  4.8 0.0 copy-start.4
  4.8 0.0 copy-start.5
  4.8 0.0 copy-start.6
  4.8 17.7 %collective-permute-start.1 = (bf16[400,128]{1,0:T(8,128)(2,1)S(1)}, bf16[400,128]{1,0:T(8,128)(2,1)S(1)}, u32[]{:S(2)}, u32[]{:S(2)}) collective-permute-start(bf16[400,128]{1,0:T(8,128)(2,1)S(1)} %get-tuple-element.14), channel_id=1, source_target_pairs={{0,191},{1,2},{2,1},{3,4},{4,3},{5,6},{6,5},{7,8},{8,7},{9,10},{10... | collective-permute-start | bytes 307208 | tf_op jit(solution)/shard_map/ppermute | solution.py:266
  22.5 0.0 collective-permute-done.ra_ref
  22.5 2.3 %collective-permute-done.1.rb_ref = bf16[400,128]{1,0:T(8,128)(2,1)S(1)} collective-permute-done((bf16[400,128]{1,0:T(8,128)(2,1)S(1)}, bf16[400,128]{1,0:T(8,128)(2,1)S(1)}, u32[]{:S(2)}, u32[]{:S(2)}) %collective-permute-start.1) | collective-permute-done | bytes 102432 | tf_op jit(solution)/shard_map/ppermute | solution.py:266
  24.9 9.9 %forecast.1 = bf16[32,128,128]{2,1,0:T(8,128)(2,1)} custom-call(bf16[128,32,128]{2,1,0:T(8,128)(2,1)S(1)} %copy-done, bf16[400,128]{1,0:T(8,128)(2,1)S(1)} %collective-permute-done.ra_ref, bf16[400,128]{1,0:T(8,128)(2,1)S(1)} %collective-permute-done.1.rb_ref, f32[32,128]{1,0:T(8,128)S(1)} %copy-done.1, f32[32,128]{1,0:T(8,128)S(1)} %copy-done.2), custom_call_target="tpu_custom_call" | custom-call | bytes 4194304 | tf_op jit(solution)/shard_map/forecast/pallas_call | solution.py:268
  34.7 4.8 %all-to-all-start = ((bf16[4,8,128,128]{3,2,1,0:T(8,128)(2,1)}), bf16[4,8,128,128]{3,2,1,0:T(8,128)(2,1)S(1)}, u32[]{:S(2)}, u32[]{:S(2)}) async-start(bf16[4,8,128,128]{3,2,1,0:T(8,128)(2,1)} %bitcast), calls=%async_computation | async-start | bytes 2097152 | tf_op jit(solution)/shard_map/all_to_all | solution.py:282
  40.2 8.8 %all-to-all-done.s_ref = bf16[4,8,128,128]{3,2,1,0:T(8,128)(2,1)S(1)} async-done(((bf16[4,8,128,128]{3,2,1,0:T(8,128)(2,1)}), bf16[4,8,128,128]{3,2,1,0:T(8,128)(2,1)S(1)}, u32[]{:S(2)}, u32[]{:S(2)}) %all-to-all-start) | async-done | bytes 1048608 | tf_op jit(solution)/shard_map/all_to_all | solution.py:282
  49.0 0.0 copy-done.3
  49.0 0.0 copy-done.4
  49.0 0.0 copy-done.5
  49.0 0.0 copy-done.6
  49.0 0.4 observe.1
  49.4 1.9 %collective-permute-start.2 = (bf16[528,256]{1,0:T(8,128)(2,1)S(1)}, bf16[528,256]{1,0:T(8,128)(2,1)S(1)}, u32[]{:S(2)}, u32[]{:S(2)}) collective-permute-start(bf16[528,256]{1,0:T(8,128)(2,1)S(1)} %get-tuple-element.15.h_ref), channel_id=1, source_target_pairs={{0,1},{1,0},{2,3},{3,2},{4,5},{5,4},{6,7},{7,6},{8,9},{9,8},{10,11... | collective-permute-start | bytes 811016 | tf_op jit(solution)/shard_map/ppermute | solution.py:293
  51.4 8.6 %collective-permute-start.3 = (bf16[528,256]{1,0:T(8,128)(2,1)S(1)}, bf16[528,256]{1,0:T(8,128)(2,1)S(1)}, u32[]{:S(2)}, u32[]{:S(2)}) collective-permute-start(bf16[528,256]{1,0:T(8,128)(2,1)S(1)} %get-tuple-element.15.h_ref), channel_id=1, source_target_pairs={{0,191},{1,2},{2,1},{3,4},{4,3},{5,6},{6,5},{7,8},{8,7},{9,10},{10... | collective-permute-start | bytes 811016 | tf_op jit(solution)/shard_map/ppermute | solution.py:292
  60.0 0.8 own.1
  60.8 0.0 collective-permute-done.2.ra_ref
  60.8 3.3 %collective-permute-done.3.rb_ref = bf16[528,256]{1,0:T(8,128)(2,1)S(1)} collective-permute-done((bf16[528,256]{1,0:T(8,128)(2,1)S(1)}, bf16[528,256]{1,0:T(8,128)(2,1)S(1)}, u32[]{:S(2)}, u32[]{:S(2)}) %collective-permute-start.3) | collective-permute-done | bytes 270368 | tf_op jit(solution)/shard_map/ppermute | solution.py:292
  64.1 2.7 %analyse.1 = bf16[4,8,128,128]{3,2,1,0:T(8,128)(2,1)S(1)} custom-call(bf16[528,256]{1,0:T(8,128)(2,1)S(1)} %collective-permute-done.2.ra_ref, bf16[528,256]{1,0:T(8,128)(2,1)S(1)} %collective-permute-done.3.rb_ref, bf16[512,1024]{1,0:T(8,128)(2,1)S(1)} %get-tuple-element.17.xb_ref, f32[8,1024]{1,0:T(8,128)S(1)} %get-tuple-element.18.xbar_ref, ...), custom_call_target="tpu_custom_call" | custom-call | flops 1342177280 | bytes 4194304 | tf_op jit(solution)/shard_map/analyse/pallas_call | solution.py:307
  66.8 13.5 %all_to_all.10 = bf16[4,8,128,128]{3,2,1,0:T(8,128)(2,1)S(1)} all-to-all(bf16[4,8,128,128]{3,2,1,0:T(8,128)(2,1)S(1)} %analyse.1), channel_id=1, replica_groups=mesh['mem'=4,'reg'=192] {'mem'}, dimensions={0} | all-to-all | bytes 2097152 | tf_op jit(solution)/shard_map/all_to_all | solution.py:315
  80.3 3.2 %place.1 = f32[128,32,128]{2,1,0:T(8,128)} custom-call(bf16[32,128,128]{2,1,0:T(8,128)(2,1)S(1)} %bitcast.2), custom_call_target="tpu_custom_call" | custom-call | tf_op jit(solution)/shard_map/place/pallas_call | solution.py:317
Async XLA Ops:
  0.0 1.2 %copy-start = (bf16[128,32,128]{2,1,0:T(8,128)(2,1)S(1)}, bf16[128,32,128]{2,1,0:T(8,128)(2,1)}, u32[]{:S(2)}) copy-start(bf16[128,32,128]{2,1,0:T(8,128)(2,1)} %x_ref.3) | copy-start | bytes 3145732
  1.2 0.7 copy-start.1
  1.9 0.7 copy-start.2
  2.8 19.7 %collective-permute-start = (bf16[400,128]{1,0:T(8,128)(2,1)S(1)}, bf16[400,128]{1,0:T(8,128)(2,1)S(1)}, u32[]{:S(2)}, u32[]{:S(2)}) collective-permute-start(bf16[400,128]{1,0:T(8,128)(2,1)S(1)} %get-tuple-element.13), channel_id=1, source_target_pairs={{0,1},{1,0},{2,3},{3,2},{4,5},{5,4},{6,7},{7,6},{8,9},{9,8},{10,11... | collective-permute-start | bytes 307208 | tf_op jit(solution)/shard_map/ppermute | solution.py:267
  4.7 44.2 %copy-start.3 = (s32[1,1,256]{2,1,0:T(1,128)S(1)}, s32[1,1,256]{2,1,0:T(1,128)}, u32[]{:S(2)}) copy-start(s32[1,1,256]{2,1,0:T(1,128)} %cell_ref.1) | copy-start | bytes 3076
  4.8 44.2 %copy-start.4 = (bf16[1,1,256]{2,1,0:T(2,128)(2,1)S(1)}, bf16[1,1,256]{2,1,0:T(2,128)(2,1)}, u32[]{:S(2)}) copy-start(bf16[1,1,256]{2,1,0:T(2,128)(2,1)} %value_ref.1) | copy-start | bytes 1540
  4.8 44.2 %copy-start.5 = (f32[1,1,256]{2,1,0:T(1,128)S(1)}, f32[1,1,256]{2,1,0:T(1,128)}, u32[]{:S(2)}) copy-start(f32[1,1,256]{2,1,0:T(1,128)} %rinv_ref.1) | copy-start | bytes 3076
  4.8 44.2 %copy-start.6 = (s32[1,1,256]{2,1,0:T(1,128)S(1)}, s32[1,1,256]{2,1,0:T(1,128)}, u32[]{:S(2)}) copy-start(s32[1,1,256]{2,1,0:T(1,128)} %loc_ref.1) | copy-start | bytes 3076
  4.8 20.1 %collective-permute-start.1 = (bf16[400,128]{1,0:T(8,128)(2,1)S(1)}, bf16[400,128]{1,0:T(8,128)(2,1)S(1)}, u32[]{:S(2)}, u32[]{:S(2)}) collective-permute-start(bf16[400,128]{1,0:T(8,128)(2,1)S(1)} %get-tuple-element.14), channel_id=1, source_target_pairs={{0,191},{1,2},{2,1},{3,4},{4,3},{5,6},{6,5},{7,8},{8,7},{9,10},{10... | collective-permute-start | bytes 307208 | tf_op jit(solution)/shard_map/ppermute | solution.py:266
  34.7 14.3 %all-to-all-start = ((bf16[4,8,128,128]{3,2,1,0:T(8,128)(2,1)}), bf16[4,8,128,128]{3,2,1,0:T(8,128)(2,1)S(1)}, u32[]{:S(2)}, u32[]{:S(2)}) async-start(bf16[4,8,128,128]{3,2,1,0:T(8,128)(2,1)} %bitcast), calls=%async_computation | async-start | bytes 2097152 | tf_op jit(solution)/shard_map/all_to_all | solution.py:282
  49.4 11.3 %collective-permute-start.2 = (bf16[528,256]{1,0:T(8,128)(2,1)S(1)}, bf16[528,256]{1,0:T(8,128)(2,1)S(1)}, u32[]{:S(2)}, u32[]{:S(2)}) collective-permute-start(bf16[528,256]{1,0:T(8,128)(2,1)S(1)} %get-tuple-element.15.h_ref), channel_id=1, source_target_pairs={{0,1},{1,0},{2,3},{3,2},{4,5},{5,4},{6,7},{7,6},{8,9},{9,8},{10,11... | collective-permute-start | bytes 811016 | tf_op jit(solution)/shard_map/ppermute | solution.py:293
  51.4 12.7 %collective-permute-start.3 = (bf16[528,256]{1,0:T(8,128)(2,1)S(1)}, bf16[528,256]{1,0:T(8,128)(2,1)S(1)}, u32[]{:S(2)}, u32[]{:S(2)}) collective-permute-start(bf16[528,256]{1,0:T(8,128)(2,1)S(1)} %get-tuple-element.15.h_ref), channel_id=1, source_target_pairs={{0,191},{1,2},{2,1},{3,4},{4,3},{5,6},{6,5},{7,8},{8,7},{9,10},{10... | collective-permute-start | bytes 811016 | tf_op jit(solution)/shard_map/ppermute | solution.py:292

commit v2 on v1

--- a/solution.py
+++ b/solution.py
@@ -6,15 +6,15 @@
 from jax.sharding import PartitionSpec as P
 
 STEPS = 3
-NSIT = 2
 LANES = 128
 BF = jnp.bfloat16
 F32 = jnp.float32
 VMEM = pl.BlockSpec(memory_space=pltpu.VMEM)
 SMEM = pl.BlockSpec(memory_space=pltpu.SMEM)
-
-
-def call(body, outs, n_in, scratch=(), specs=None, flops=0, moved=0, name=None):
+HBM = pl.BlockSpec(memory_space=pltpu.HBM)
+
+
+def call(body, outs, n_in, scratch=(), specs=None, flops=0, moved=0, grant=40 << 20):
     return pl.pallas_call(
         body,
         out_shape=[jax.ShapeDtypeStruct(s, d) for s, d in outs],
@@ -22,26 +22,39 @@
         out_specs=[VMEM] * len(outs),
         scratch_shapes=list(scratch),
         cost_estimate=pl.CostEstimate(flops=flops, bytes_accessed=moved, transcendentals=0),
-        compiler_params=pltpu.CompilerParams(vmem_limit_bytes=40 << 20),
-        name=name,
-    )
-
-
-def pack_body(x_ref, d_ref, a_ref, sa_ref, sb_ref, rows, coef):
+        compiler_params=pltpu.CompilerParams(vmem_limit_bytes=grant),
+    )
+
+
+def pack_body(
+    x_ref, d_ref, a_ref, sa_ref, sb_ref, xv_ref, dv_ref, av_ref, head, tail, rows, coef, sems
+):
     members = x_ref.shape[0]
     lines = x_ref.shape[1]
-
-    def edge(out_ref, tail):
-        base = lines - 8 if tail else 0
-        rows[...] = x_ref[:, base : base + 8, :].astype(F32).reshape(members * 8, LANES)
-        first = 8 - STEPS if tail else 0
+    last = lines - 8
+    copies = [
+        pltpu.make_async_copy(x_ref.at[:, pl.ds(0, 8), :], head, sems.at[0]),
+        pltpu.make_async_copy(x_ref.at[:, pl.ds(last, 8), :], tail, sems.at[1]),
+        pltpu.make_async_copy(d_ref, dv_ref, sems.at[2]),
+        pltpu.make_async_copy(a_ref, av_ref, sems.at[3]),
+    ]
+    whole_copy = pltpu.make_async_copy(x_ref, xv_ref, sems.at[4])
+    for copy in copies:
+        copy.start()
+    whole_copy.start()
+    for copy in copies:
+        copy.wait()
+
+    def edge(out_ref, source, side):
+        rows[...] = source[...].astype(F32).reshape(members * 8, LANES)
+        first = (8 - STEPS) * side
         for k in range(STEPS):
             out_ref[k * members : (k + 1) * members, :] = rows[
                 pl.ds(first + k, members, stride=8), :
             ].astype(BF)
-        at = lines - 2 if tail else 0
-        coef[0:2, :] = d_ref[at : at + 2, :]
-        coef[2:4, :] = a_ref[at : at + 2, :]
+        at = (lines - 2) * side
+        coef[0:2, :] = dv_ref[at : at + 2, :]
+        coef[2:4, :] = av_ref[at : at + 2, :]
         whole = coef[0:4, :]
         high = whole.astype(BF).astype(F32)
         middle = (whole - high).astype(BF).astype(F32)
@@ -55,23 +68,101 @@
 
     @pl.when(even)
     def _():
-        edge(sa_ref, True)
-        edge(sb_ref, False)
+        edge(sa_ref, tail, 1)
+        edge(sb_ref, head, 0)
 
     @pl.when(jnp.logical_not(even))
     def _():
-        edge(sa_ref, False)
-        edge(sb_ref, True)
-
-
-def forecast_body(x_ref, ra_ref, rb_ref, d_ref, a_ref, o_ref, xs, halo, dd, aa, cf):
+        edge(sa_ref, head, 0)
+        edge(sb_ref, tail, 1)
+
+    whole_copy.wait()
+
+
+def laplace():
+    i = lax.broadcasted_iota(jnp.int32, (LANES, LANES), 0)
+    j = lax.broadcasted_iota(jnp.int32, (LANES, LANES), 1)
+    gap = jnp.bitwise_and(i - j, LANES - 1)
+    beside = jnp.logical_or(gap == 1, gap == LANES - 1)
+    return jnp.where(gap == 0, -4.0, jnp.where(beside, 1.0, 0.0)).astype(BF)
+
+
+def sides_of(centre):
+    return pltpu.roll(centre, 1, 1) + pltpu.roll(centre, LANES - 1, 1)
+
+
+KEEP = ((0, 0), (0, 1), ("lap", 0), (1, 1), (1, 2), (2, 2), (2, 3))
+
+
+def interior_body(x_ref, d_ref, a_ref, o_ref, k_ref, xs, ls, cf):
     members = x_ref.shape[0]
     lines = x_ref.shape[1]
+    for row in range(lines):
+        dif = jnp.broadcast_to(d_ref[row : row + 1, :], (8, LANES))
+        adv = 0.5 * jnp.broadcast_to(a_ref[row : row + 1, :], (8, LANES))
+        cf[row, 0:8, :] = 1.0 - 4.0 * dif
+        cf[row, 8:16, :] = dif
+        cf[row, 16:24, :] = dif + adv
+        cf[row, 24:32, :] = dif - adv
+    across = laplace()
+    block = 16
+
+    def step(b, carry):
+        here = pl.ds(pl.multiple_of(b * block, block), block)
+        for q in range(lines // 8):
+            part = x_ref[here, 8 * q : 8 * q + 8, :].astype(F32).reshape(block * 8, LANES)
+            xs[q] = part
+            ls[q] = jnp.dot(part.astype(BF), across, preferred_element_type=F32)
+
+        def c(row, k):
+            v = cf[row, 8 * k : 8 * k + 8, :]
+            return jnp.concatenate([v, v], axis=0)
+
+        def keep(what, row, value):
+            for side in range(2):
+                away = lines - 1 - row if side else row
+                if (what, away) in KEEP:
+                    k_ref[side * len(KEEP) + KEEP.index((what, away)), here, :] = value
+
+        levels = [{} for _ in range(STEPS + 1)]
+        for row in range(lines):
+            at_row = pl.ds(row % 8, block, stride=8)
+            levels[0][row] = xs[row // 8, at_row, :]
+            keep(0, row, levels[0][row])
+            if row in (0, lines - 1):
+                keep("lap", row, ls[row // 8, at_row, :])
+            for level in range(1, STEPS + 1):
+                at = row - level
+                if at < level or at + level >= lines:
+                    continue
+                prev = levels[level - 1]
+                centre = prev[at]
+                vertical = c(at, 2) * prev[at - 1] + c(at, 3) * prev[at + 1]
+                if level == 1:
+                    lap = ls[at // 8, pl.ds(at % 8, block, stride=8), :]
+                    new = centre + c(at, 1) * lap + vertical
+                else:
+                    new = c(at, 0) * centre + c(at, 1) * sides_of(centre) + vertical
+                keep(level, at, new)
+                if level == STEPS:
+                    o_ref[at, here, :] = new.astype(BF)
+                else:
+                    levels[level][at] = new
+                del prev[at - 1]
+        return carry
+
+    lax.fori_loop(0, members // block, step, 0)
+
+
+def edge_body(f_ref, k_ref, ra_ref, rb_ref, d_ref, a_ref, o_ref, halo, dd, aa, new_rows, sems):
+    del f_ref
+    members = k_ref.shape[1]
+    lines = d_ref.shape[0]
     reach = STEPS * members
     even = lax.rem(lax.axis_index("reg"), 2) == 0
 
     def take(ref, side):
-        halo[side * reach : (side + 1) * reach, :] = ref[0:reach, :].astype(F32)
+        halo[side * reach : (side + 1) * reach, :] = ref[0:reach, :]
         parts = ref[reach:, :].astype(F32)
         whole = parts[0:4] + parts[4:8] + parts[8:12]
         at = (lines + 2) if side else 0
@@ -90,51 +181,65 @@
 
     dd[2 : 2 + lines, :] = d_ref[...]
     aa[2 : 2 + lines, :] = a_ref[...]
-    for row in range(lines + 4):
-        dif = jnp.broadcast_to(dd[row : row + 1, :], (8, LANES))
-        adv = 0.5 * jnp.broadcast_to(aa[row : row + 1, :], (8, LANES))
-        cf[row, 0:8, :] = 1.0 - 4.0 * dif
-        cf[row, 8:16, :] = dif
-        cf[row, 16:24, :] = dif + adv
-        cf[row, 24:32, :] = dif - adv
-
-    block = 16
-
-    def step(b, carry):
-        xs[...] = x_ref[pl.ds(b * block, block)].astype(F32).reshape(block * lines, LANES)
-
-        def start_row(row):
-            if row < 0:
-                return halo[pl.ds((row + STEPS) * members + b * block, block), :]
-            if row >= lines:
-                return halo[pl.ds(reach + (row - lines) * members + b * block, block), :]
-            return xs[pl.ds(row, block, stride=lines), :]
-
-        def update(row, north, centre, south):
-            def c(k):
-                v = cf[row + 2, 8 * k : 8 * k + 8, :]
-                return jnp.concatenate([v, v], axis=0)
-
-            sides = pltpu.roll(centre, 1, 1) + pltpu.roll(centre, LANES - 1, 1)
-            return c(0) * centre + c(1) * sides + c(2) * north + c(3) * south
-
-        levels = [{} for _ in range(STEPS + 1)]
-        for row in range(-STEPS, lines + STEPS):
-            levels[0][row] = start_row(row)
-            for level in range(1, STEPS + 1):
-                at = row - level
-                prev = levels[level - 1]
-                if at - 1 not in prev or at < level - STEPS:
-                    continue
-                new = update(at, prev[at - 1], prev[at], prev[at + 1])
+    across = laplace()
+    copies = []
+    for side in range(2):
+
+        def at(away):
+            return lines - 1 - away if side else away
+
+        def coefs(away):
+            row = at(away) + 2
+            dif = jnp.broadcast_to(dd[row : row + 1, :], (members, LANES))
+            adv = 0.5 * jnp.broadcast_to(aa[row : row + 1, :], (members, LANES))
+            inward = dif - adv if side == 0 else dif + adv
+            outward = dif + adv if side == 0 else dif - adv
+            return dif, outward, inward
+
+        def outer(away):
+            k = (-away - 1) if side else (STEPS + away)
+            start = side * reach + k * members
+            return halo[start : start + members, :]
+
+        def kept(what, away):
+            return k_ref[side * len(KEEP) + KEEP.index((what, away))]
+
+        states = [{} for _ in range(STEPS)]
+        for away in range(-STEPS, 0):
+            states[0][away] = outer(away).astype(F32)
+        for what, away in KEEP:
+            if what != "lap":
+                states[what][away] = kept(what, away)
+        for level in range(1, STEPS + 1):
+            prev = states[level - 1]
+            for away in range(level - STEPS, level):
+                dif, outward, inward = coefs(away)
+                vertical = outward * prev[away - 1] + inward * prev[away + 1]
+                centre = prev[away]
+                if level == 1:
+                    lap = (
+                        kept("lap", 0)
+                        if away == 0
+                        else jnp.dot(outer(away), across, preferred_element_type=F32)
+                    )
+                    new = centre + dif * lap + vertical
+                else:
+                    new = (1.0 - 4.0 * dif) * centre + dif * sides_of(centre) + vertical
                 if level == STEPS:
-                    o_ref[at, pl.ds(b * block, block), :] = new.astype(BF)
+                    slot = STEPS - 1 - away if side else away
+                    new_rows[side * STEPS + slot] = new.astype(BF)
                 else:
-                    levels[level][at] = new
-                del prev[at - 1]
-        return carry
-
-    lax.fori_loop(0, members // block, step, 0)
+                    states[level][away] = new
+        first = lines - STEPS if side else 0
+        copy = pltpu.make_async_copy(
+            new_rows.at[pl.ds(side * STEPS, STEPS)],
+            o_ref.at[pl.ds(first, STEPS)],
+            sems.at[side],
+        )
+        copy.start()
+        copies.append(copy)
+    for copy in copies:
+        copy.wait()
 
 
 def observe_body(s_ref, cell_ref, value_ref, rinv_ref, count_ref, loc_ref, h_ref, prec_ref):
@@ -236,15 +341,14 @@
 def place_body(r_ref, o_ref, out):
     lines = r_ref.shape[0]
     block = o_ref.shape[0]
-    b = pl.program_id(0)
+    here = pl.ds(pl.multiple_of(pl.program_id(0) * block, block), block)
     for row in range(lines):
-        out[pl.ds(row, block, stride=lines), :] = r_ref[
-            row, pl.ds(pl.multiple_of(b * block, block), block), :
-        ].astype(F32)
-    o_ref[...] = out[...].reshape(block, lines, LANES)
-
-
-def on_device(members, diffusivity, advection, obs_value, obs_rinv, obs_cell, obs_count, loc_index):
+        out[row // 8, pl.ds(row % 8, block, stride=8), :] = r_ref[row, here, :].astype(F32)
+    for q in range(lines // 8):
+        o_ref[:, 8 * q : 8 * q + 8, :] = out[q].reshape(block, 8, LANES)
+
+
+def program(members, diffusivity, advection, obs_value, obs_rinv, obs_cell, obs_count, loc_index):
     per, lines, _ = members.shape
     groups = lax.axis_size("mem")
     regions = lax.axis_size("reg")
@@ -254,31 +358,57 @@
     near = [(i, i ^ 1) for i in range(regions)]
     across = [(i, (i + 1) % regions if i % 2 else (i - 1) % regions) for i in range(regions)]
 
-    edge = ((STEPS * per + 16, LANES), BF)
-    send_a, send_b = call(
+    reach = STEPS * per + 16
+    send_a, send_b, members, diffusivity, advection = call(
         pack_body,
-        [edge, edge],
+        [((reach, LANES), BF)] * 2
+        + [(v.shape, v.dtype) for v in (members, diffusivity, advection)],
         3,
-        [pltpu.VMEM((per * 8, LANES), F32), pltpu.VMEM((16, LANES), F32)],
+        [
+            pltpu.VMEM((per, 8, LANES), BF),
+            pltpu.VMEM((per, 8, LANES), BF),
+            pltpu.VMEM((per * 8, LANES), F32),
+            pltpu.VMEM((16, LANES), F32),
+            pltpu.SemaphoreType.DMA((5,)),
+        ],
+        specs=[HBM, HBM, HBM],
         moved=1 << 20,
-        name="pack",
-    )(members, diffusivity, advection)
+    )(
+        *[
+            pltpu.with_memory_space_constraint(v, pltpu.HBM)
+            for v in (members, diffusivity, advection)
+        ]
+    )
     got_b = lax.ppermute(send_b, "reg", across)
     got_a = lax.ppermute(send_a, "reg", near)
-    (ahead,) = call(
-        forecast_body,
-        [((lines, per, LANES), BF)],
-        5,
+    inner, kept = call(
+        interior_body,
+        [((lines, per, LANES), BF), ((2 * len(KEEP), per, LANES), F32)],
+        3,
         [
-            pltpu.VMEM((16 * lines, LANES), F32),
-            pltpu.VMEM((2 * STEPS * per, LANES), F32),
+            pltpu.VMEM((lines // 8, 16 * 8, LANES), F32),
+            pltpu.VMEM((lines // 8, 16 * 8, LANES), F32),
+            pltpu.VMEM((lines, 32, LANES), F32),
+        ],
+        moved=12 << 20,
+    )(members, diffusivity, advection)
+    ahead = pl.pallas_call(
+        edge_body,
+        out_shape=jax.ShapeDtypeStruct((lines, per, LANES), BF),
+        in_specs=[pl.BlockSpec(memory_space=pl.ANY)] + [VMEM] * 5,
+        out_specs=pl.BlockSpec(memory_space=pl.ANY),
+        input_output_aliases={0: 0},
+        scratch_shapes=[
+            pltpu.VMEM((2 * STEPS * per, LANES), BF),
             pltpu.VMEM((lines + 8, LANES), F32),
             pltpu.VMEM((lines + 8, LANES), F32),
-            pltpu.VMEM((lines + 4, 32, LANES), F32),
+            pltpu.VMEM((2 * STEPS, per, LANES), BF),
+            pltpu.SemaphoreType.DMA((2,)),
         ],
-        moved=4 << 20,
-        name="forecast",
-    )(members, got_a, got_b, diffusivity, advection)
+        cost_estimate=pl.CostEstimate(flops=0, bytes_accessed=2 << 20, transcendentals=0),
+        compiler_params=pltpu.CompilerParams(vmem_limit_bytes=40 << 20),
+        name="edge",
+    )(inner, kept, got_a, got_b, diffusivity, advection)
     states = lax.all_to_all(ahead.reshape(groups, tile, per, LANES), "mem", 0, 0)
     obs, prec = call(
         observe_body,
@@ -287,7 +417,6 @@
         specs=[VMEM, VMEM, VMEM, VMEM, SMEM, VMEM],
         flops=2 * total * tile * LANES * slots,
         moved=2 << 20,
-        name="observe",
     )(states, obs_cell, obs_value, obs_rinv, obs_count, loc_index)
     nb = lax.ppermute(obs, "reg", across)
     na = lax.ppermute(obs, "reg", near)
@@ -302,7 +431,6 @@
         3,
         flops=2 * total * total * slots,
         moved=4 << 20,
-        name="own",
     )(states, obs, prec)
     (back,) = call(
         analyse_body,
@@ -310,7 +438,6 @@
         6,
         flops=10 * total * total * total,
         moved=4 << 20,
-        name="analyse",
     )(na, nb, xb, xbar, system, force)
     home = lax.all_to_all(back, "mem", 0, 0).reshape(lines, per, LANES)
     block = 32
@@ -320,7 +447,7 @@
         out_shape=jax.ShapeDtypeStruct((per, lines, LANES), F32),
         in_specs=[VMEM],
         out_specs=pl.BlockSpec((block, lines, LANES), lambda i: (i, 0, 0)),
-        scratch_shapes=[pltpu.VMEM((block * lines, LANES), F32)],
+        scratch_shapes=[pltpu.VMEM((lines // 8, block * 8, LANES), F32)],
         compiler_params=pltpu.CompilerParams(vmem_limit_bytes=40 << 20),
         name="place",
     )(home)
@@ -328,7 +455,7 @@
 
 def solution(mesh):
     return jax.shard_map(
-        on_device,
+        program,
         mesh=mesh,
         in_specs=(
             P("mem", "reg", None),

time: 83.9 us -> 75.4 us (0.90)
  Pallas kernels: 17.1 us -> 13.8 us
  local copies, waits for them, and re-layouts: 2.68 us -> 0.02 us
  waiting for transfers between devices: 14.4 us -> 12.1 us
    pallas_call x6 -> x7, Pallas kernels: 17.1 us -> 13.8 us  [the longest x1 5 us: program(): call(interior_body, [((lines, per, LANES), BF), ((2 * len(KEEP), per, LAN...]
    unnamed x14 -> x8, local copies, waits for them, and re-layouts: 2.68 us -> 0.02 us
    ppermute x4, waiting for transfers between devices: 5.62 us -> 3.31 us  [the longest x1 3.3 us: program(): nb = lax.ppermute(obs, 'reg', across)]
  transfers between devices with their start and end apart: 5 -> 5, of which waited for: 3 -> 2; matrix products, arithmetic and copies ran while one was open for 0% -> 0% of each run, Pallas kernels for 1% -> 8%
where the time goes in v2:
time: 75.4 us; the launch traced here: 75.1 us
  starting transfers between devices  35.1 us (47%)
  Pallas kernels  13.8 us (18%)
  blocking collectives  13.3 us (18%)
  waiting for transfers between devices  12.1 us (16%)
  between operations  0.77 us (1%)
    ppermute x1, starting transfers between devices, program(): got_b = lax.ppermute(send_b, 'reg', across)  17.6 us
    all_to_all x1, blocking collectives, program(): home = lax.all_to_all(back, 'mem', 0, 0).reshape(lines, per, LANES)  13.3 us
    ppermute x1, starting transfers between devices, program(): nb = lax.ppermute(obs, 'reg', across)  8.83 us
    all_to_all x1, waiting for transfers between devices, program(): lax.all_to_all(ahead.reshape(groups, tile, per, LANES), 'mem', 0, 0)  8.78 us
    pallas_call x1, Pallas kernels, program(): call(interior_body, [((lines, per, LANES), BF), ((2 * len(KEEP), per, LAN...  5 us
    all_to_all x1, starting transfers between devices, program(): lax.all_to_all(ahead.reshape(groups, tile, per, LANES), 'mem', 0, 0)  4.84 us
    ppermute x1, waiting for transfers between devices, program(): nb = lax.ppermute(obs, 'reg', across)  3.3 us
    pallas_call x1, Pallas kernels, program(): call(analyse_body, [((groups, tile, per, LANES), BF)], 6, flops=10 * tota...  2.66 us
  transfers between devices with their start and end apart: 5, of which 2 were waited for; matrix products, arithmetic and copies ran while one was open for 0% of the time, Pallas kernels for 8%

profile of v2, /device:TPU:2, one launch (start us, length us, event | category | flops | bytes accessed | tf_op | source)
XLA Modules:
  0.0 75.1 jit_solution(378836055729339315)
XLA Ops:
  0.0 1.5 %shard_map.82 = (bf16[400,128]{1,0:T(8,128)(2,1)S(1)}, bf16[400,128]{1,0:T(8,128)(2,1)S(1)}, bf16[128,32,128]{2,1,0:T(8,128)(2,1)S(1)}, f32[32,128]{1,0:T(8,128)S(1)}, f32[32,128]{1,0:T(8,128)S(1)}) custom-call(bf16[128,32,128]{2,1,0:T(8,128)(2,1)} %x_ref.1, f32[32,128]{1,0:T(8,128)} %d_ref.1, f32[32,128]{1,0:T(8,128)} %a_ref.1), custom_call_target="tpu_custom_call" | custom-call | bytes 1048576 | tf_op jit(solution)/shard_map/pallas_call | solution.py:362
  1.5 1.9 %collective-permute-start = (bf16[400,128]{1,0:T(8,128)(2,1)S(1)}, bf16[400,128]{1,0:T(8,128)(2,1)S(1)}, u32[]{:S(2)}, u32[]{:S(2)}) collective-permute-start(bf16[400,128]{1,0:T(8,128)(2,1)S(1)} %get-tuple-element.23), channel_id=1, source_target_pairs={{0,1},{1,0},{2,3},{3,2},{4,5},{5,4},{6,7},{7,6},{8,9},{9,8},{10,11... | collective-permute-start | bytes 307208 | tf_op jit(solution)/shard_map/ppermute | solution.py:383
  3.4 17.6 %collective-permute-start.1 = (bf16[400,128]{1,0:T(8,128)(2,1)S(1)}, bf16[400,128]{1,0:T(8,128)(2,1)S(1)}, u32[]{:S(2)}, u32[]{:S(2)}) collective-permute-start(bf16[400,128]{1,0:T(8,128)(2,1)S(1)} %get-tuple-element.24), channel_id=1, source_target_pairs={{0,191},{1,2},{2,1},{3,4},{4,3},{5,6},{6,5},{7,8},{8,7},{9,10},{10... | collective-permute-start | bytes 307208 | tf_op jit(solution)/shard_map/ppermute | solution.py:382
  21.0 5.0 %shard_map.83 = (bf16[32,128,128]{2,1,0:T(8,128)(2,1)}, f32[14,128,128]{2,1,0:T(8,128)S(1)}) custom-call(bf16[128,32,128]{2,1,0:T(8,128)(2,1)S(1)} %get-tuple-element.18.x_ref, f32[32,128]{1,0:T(8,128)S(1)} %get-tuple-element.19.d_ref, f32[32,128]{1,0:T(8,128)S(1)} %get-tuple-element.20.a_ref), custom_call_target="tpu_custom_call" | custom-call | bytes 12582912 | tf_op jit(solution)/shard_map/pallas_call | solution.py:384
  26.0 0.0 collective-permute-done.ra_ref
  26.0 0.0 collective-permute-done.1.rb_ref
  26.0 0.0 copy-start
  26.0 0.0 copy-start.1
  26.0 0.0 copy-start.2
  26.1 0.0 copy-start.3
  26.1 1.3 %edge.1 = bf16[32,128,128]{2,1,0:T(8,128)(2,1)} custom-call(bf16[32,128,128]{2,1,0:T(8,128)(2,1)} %get-tuple-element.21.f_ref, f32[14,128,128]{2,1,0:T(8,128)S(1)} %get-tuple-element.22.k_ref, bf16[400,128]{1,0:T(8,128)(2,1)S(1)} %collective-permute-done.ra_ref, bf16[400,128]{1,0:T(8,128)(2,1)S(1)} %collective-permute-done.1.rb_ref, ...), custom_call_target="tpu_custom_call", output_to_operand_aliasing={{}: (0, {})} | custom-call | bytes 2097152 | tf_op jit(solution)/shard_map/edge/pallas_call | solution.py:395
  27.4 4.8 %all-to-all-start = ((bf16[4,8,128,128]{3,2,1,0:T(8,128)(2,1)}), bf16[4,8,128,128]{3,2,1,0:T(8,128)(2,1)S(1)}, u32[]{:S(2)}, u32[]{:S(2)}) async-start(bf16[4,8,128,128]{3,2,1,0:T(8,128)(2,1)} %bitcast), calls=%async_computation | async-start | bytes 2097152 | tf_op jit(solution)/shard_map/all_to_all | solution.py:412
  32.9 8.8 %all-to-all-done.s_ref = bf16[4,8,128,128]{3,2,1,0:T(8,128)(2,1)S(1)} async-done(((bf16[4,8,128,128]{3,2,1,0:T(8,128)(2,1)}), bf16[4,8,128,128]{3,2,1,0:T(8,128)(2,1)S(1)}, u32[]{:S(2)}, u32[]{:S(2)}) %all-to-all-start) | async-done | bytes 1048608 | tf_op jit(solution)/shard_map/all_to_all | solution.py:412
  41.6 0.0 copy-done
  41.7 0.0 copy-done.1
  41.7 0.0 copy-done.2
  41.7 0.0 copy-done.3
  41.7 0.4 shard_map.84
  42.1 1.9 %collective-permute-start.2 = (bf16[528,256]{1,0:T(8,128)(2,1)S(1)}, bf16[528,256]{1,0:T(8,128)(2,1)S(1)}, u32[]{:S(2)}, u32[]{:S(2)}) collective-permute-start(bf16[528,256]{1,0:T(8,128)(2,1)S(1)} %get-tuple-element.25.h_ref), channel_id=1, source_target_pairs={{0,1},{1,0},{2,3},{3,2},{4,5},{5,4},{6,7},{7,6},{8,9},{9,8},{10,11... | collective-permute-start | bytes 811016 | tf_op jit(solution)/shard_map/ppermute | solution.py:422
  44.0 8.8 %collective-permute-start.3 = (bf16[528,256]{1,0:T(8,128)(2,1)S(1)}, bf16[528,256]{1,0:T(8,128)(2,1)S(1)}, u32[]{:S(2)}, u32[]{:S(2)}) collective-permute-start(bf16[528,256]{1,0:T(8,128)(2,1)S(1)} %get-tuple-element.25.h_ref), channel_id=1, source_target_pairs={{0,191},{1,2},{2,1},{3,4},{4,3},{5,6},{6,5},{7,8},{8,7},{9,10},{10... | collective-permute-start | bytes 811016 | tf_op jit(solution)/shard_map/ppermute | solution.py:421
  52.9 0.8 %shard_map.85 = (bf16[512,1024]{1,0:T(8,128)(2,1)S(1)}, f32[8,1024]{1,0:T(8,128)S(1)}, f32[512,512]{1,0:T(8,128)S(1)}, f32[512,128]{1,0:T(8,128)S(1)}) custom-call(bf16[4,8,128,128]{3,2,1,0:T(8,128)(2,1)S(1)} %all-to-all-done.s_ref, bf16[528,256]{1,0:T(8,128)(2,1)S(1)} %get-tuple-element.25.h_ref, f32[8,256]{1,0:T(8,128)S(1)} %get-tuple-element.26.prec_ref), custom_call_target="tpu_custom_call" | custom-call | flops 134217728 | bytes 4194304 | tf_op jit(solution)/shard_map/pallas_call | solution.py:423
  53.7 0.0 collective-permute-done.2.ra_ref
  53.7 3.3 %collective-permute-done.3.rb_ref = bf16[528,256]{1,0:T(8,128)(2,1)S(1)} collective-permute-done((bf16[528,256]{1,0:T(8,128)(2,1)S(1)}, bf16[528,256]{1,0:T(8,128)(2,1)S(1)}, u32[]{:S(2)}, u32[]{:S(2)}) %collective-permute-start.3) | collective-permute-done | bytes 270368 | tf_op jit(solution)/shard_map/ppermute | solution.py:421
  57.0 2.7 %shard_map.86 = bf16[4,8,128,128]{3,2,1,0:T(8,128)(2,1)S(1)} custom-call(bf16[528,256]{1,0:T(8,128)(2,1)S(1)} %collective-permute-done.2.ra_ref, bf16[528,256]{1,0:T(8,128)(2,1)S(1)} %collective-permute-done.3.rb_ref, bf16[512,1024]{1,0:T(8,128)(2,1)S(1)} %get-tuple-element.27.xb_ref, f32[8,1024]{1,0:T(8,128)S(1)} %get-tuple-element.28.xbar_ref, ...), custom_call_target="tpu_custom_call" | custom-call | flops 1342177280 | bytes 4194304 | tf_op jit(solution)/shard_map/pallas_call | solution.py:435
  59.7 13.3 %all_to_all.10 = bf16[4,8,128,128]{3,2,1,0:T(8,128)(2,1)S(1)} all-to-all(bf16[4,8,128,128]{3,2,1,0:T(8,128)(2,1)S(1)} %shard_map.86), channel_id=1, replica_groups=mesh['mem'=4,'reg'=192] {'mem'}, dimensions={0} | all-to-all | bytes 2097152 | tf_op jit(solution)/shard_map/all_to_all | solution.py:442
  73.0 2.1 %place.1 = f32[128,32,128]{2,1,0:T(8,128)} custom-call(bf16[32,128,128]{2,1,0:T(8,128)(2,1)S(1)} %bitcast.2), custom_call_target="tpu_custom_call" | custom-call | tf_op jit(solution)/shard_map/place/pallas_call | solution.py:444
Async XLA Ops:
  1.5 24.5 %collective-permute-start = (bf16[400,128]{1,0:T(8,128)(2,1)S(1)}, bf16[400,128]{1,0:T(8,128)(2,1)S(1)}, u32[]{:S(2)}, u32[]{:S(2)}) collective-permute-start(bf16[400,128]{1,0:T(8,128)(2,1)S(1)} %get-tuple-element.23), channel_id=1, source_target_pairs={{0,1},{1,0},{2,3},{3,2},{4,5},{5,4},{6,7},{7,6},{8,9},{9,8},{10,11... | collective-permute-start | bytes 307208 | tf_op jit(solution)/shard_map/ppermute | solution.py:383
  3.4 22.6 %collective-permute-start.1 = (bf16[400,128]{1,0:T(8,128)(2,1)S(1)}, bf16[400,128]{1,0:T(8,128)(2,1)S(1)}, u32[]{:S(2)}, u32[]{:S(2)}) collective-permute-start(bf16[400,128]{1,0:T(8,128)(2,1)S(1)} %get-tuple-element.24), channel_id=1, source_target_pairs={{0,191},{1,2},{2,1},{3,4},{4,3},{5,6},{6,5},{7,8},{8,7},{9,10},{10... | collective-permute-start | bytes 307208 | tf_op jit(solution)/shard_map/ppermute | solution.py:382
  26.0 15.6 %copy-start = (s32[1,1,256]{2,1,0:T(1,128)S(1)}, s32[1,1,256]{2,1,0:T(1,128)}, u32[]{:S(2)}) copy-start(s32[1,1,256]{2,1,0:T(1,128)} %cell_ref.1) | copy-start | bytes 3076
  26.0 15.6 %copy-start.1 = (bf16[1,1,256]{2,1,0:T(2,128)(2,1)S(1)}, bf16[1,1,256]{2,1,0:T(2,128)(2,1)}, u32[]{:S(2)}) copy-start(bf16[1,1,256]{2,1,0:T(2,128)(2,1)} %value_ref.1) | copy-start | bytes 1540
  26.0 15.6 %copy-start.2 = (f32[1,1,256]{2,1,0:T(1,128)S(1)}, f32[1,1,256]{2,1,0:T(1,128)}, u32[]{:S(2)}) copy-start(f32[1,1,256]{2,1,0:T(1,128)} %rinv_ref.1) | copy-start | bytes 3076
  26.1 15.6 %copy-start.3 = (s32[1,1,256]{2,1,0:T(1,128)S(1)}, s32[1,1,256]{2,1,0:T(1,128)}, u32[]{:S(2)}) copy-start(s32[1,1,256]{2,1,0:T(1,128)} %loc_ref.1) | copy-start | bytes 3076
  27.4 14.3 %all-to-all-start = ((bf16[4,8,128,128]{3,2,1,0:T(8,128)(2,1)}), bf16[4,8,128,128]{3,2,1,0:T(8,128)(2,1)S(1)}, u32[]{:S(2)}, u32[]{:S(2)}) async-start(bf16[4,8,128,128]{3,2,1,0:T(8,128)(2,1)} %bitcast), calls=%async_computation | async-start | bytes 2097152 | tf_op jit(solution)/shard_map/all_to_all | solution.py:412
  42.1 11.6 %collective-permute-start.2 = (bf16[528,256]{1,0:T(8,128)(2,1)S(1)}, bf16[528,256]{1,0:T(8,128)(2,1)S(1)}, u32[]{:S(2)}, u32[]{:S(2)}) collective-permute-start(bf16[528,256]{1,0:T(8,128)(2,1)S(1)} %get-tuple-element.25.h_ref), channel_id=1, source_target_pairs={{0,1},{1,0},{2,3},{3,2},{4,5},{5,4},{6,7},{7,6},{8,9},{9,8},{10,11... | collective-permute-start | bytes 811016 | tf_op jit(solution)/shard_map/ppermute | solution.py:422
  44.0 13.0 %collective-permute-start.3 = (bf16[528,256]{1,0:T(8,128)(2,1)S(1)}, bf16[528,256]{1,0:T(8,128)(2,1)S(1)}, u32[]{:S(2)}, u32[]{:S(2)}) collective-permute-start(bf16[528,256]{1,0:T(8,128)(2,1)S(1)} %get-tuple-element.25.h_ref), channel_id=1, source_target_pairs={{0,191},{1,2},{2,1},{3,4},{4,3},{5,6},{6,5},{7,8},{8,7},{9,10},{10... | collective-permute-start | bytes 811016 | tf_op jit(solution)/shard_map/ppermute | solution.py:421

commit v3 on v2

--- a/solution.py
+++ b/solution.py
@@ -7,6 +7,7 @@
 
 STEPS = 3
 LANES = 128
+BLOCK = 32
 BF = jnp.bfloat16
 F32 = jnp.float32
 VMEM = pl.BlockSpec(memory_space=pltpu.VMEM)
@@ -87,8 +88,23 @@
     return jnp.where(gap == 0, -4.0, jnp.where(beside, 1.0, 0.0)).astype(BF)
 
 
-def sides_of(centre):
+def beside():
+    i = lax.broadcasted_iota(jnp.int32, (LANES, LANES), 0)
+    j = lax.broadcasted_iota(jnp.int32, (LANES, LANES), 1)
+    gap = jnp.bitwise_and(i - j, LANES - 1)
+    once = jnp.where(jnp.logical_or(gap == 1, gap == LANES - 1), 1.0, 0.0).astype(BF)
+    return jnp.concatenate([once, once], axis=0)
+
+
+def rolled(centre):
     return pltpu.roll(centre, 1, 1) + pltpu.roll(centre, LANES - 1, 1)
+
+
+def sides_of(centre, pair):
+    high = centre.astype(BF)
+    low = (centre - high.astype(F32)).astype(BF)
+    both = jnp.concatenate([high, low], axis=1)
+    return jnp.dot(both, pair, preferred_element_type=F32)
 
 
 KEEP = ((0, 0), (0, 1), ("lap", 0), (1, 1), (1, 2), (2, 2), (2, 3))
@@ -105,18 +121,22 @@
         cf[row, 16:24, :] = dif + adv
         cf[row, 24:32, :] = dif - adv
     across = laplace()
-    block = 16
-
-    def step(b, carry):
-        here = pl.ds(pl.multiple_of(b * block, block), block)
+    pair = beside()
+    block = BLOCK
+
+    def stage(b, slot):
+        here = pl.ds(b * block, block)
         for q in range(lines // 8):
             part = x_ref[here, 8 * q : 8 * q + 8, :].astype(F32).reshape(block * 8, LANES)
-            xs[q] = part
-            ls[q] = jnp.dot(part.astype(BF), across, preferred_element_type=F32)
-
-        def c(row, k):
-            v = cf[row, 8 * k : 8 * k + 8, :]
-            return jnp.concatenate([v, v], axis=0)
+            xs[slot, q] = part
+            ls[slot, q] = jnp.dot(part.astype(BF), across, preferred_element_type=F32)
+
+    def c(row, k):
+        v = cf[row, 8 * k : 8 * k + 8, :]
+        return jnp.concatenate([v] * (block // 8), axis=0)
+
+    def advance(b, slot):
+        here = pl.ds(b * block, block)
 
         def keep(what, row, value):
             for side in range(2):
@@ -127,10 +147,10 @@
         levels = [{} for _ in range(STEPS + 1)]
         for row in range(lines):
             at_row = pl.ds(row % 8, block, stride=8)
-            levels[0][row] = xs[row // 8, at_row, :]
+            levels[0][row] = xs[slot, row // 8, at_row, :]
             keep(0, row, levels[0][row])
             if row in (0, lines - 1):
-                keep("lap", row, ls[row // 8, at_row, :])
+                keep("lap", row, ls[slot, row // 8, at_row, :])
             for level in range(1, STEPS + 1):
                 at = row - level
                 if at < level or at + level >= lines:
@@ -139,23 +159,28 @@
                 centre = prev[at]
                 vertical = c(at, 2) * prev[at - 1] + c(at, 3) * prev[at + 1]
                 if level == 1:
-                    lap = ls[at // 8, pl.ds(at % 8, block, stride=8), :]
+                    lap = ls[slot, at // 8, pl.ds(at % 8, block, stride=8), :]
                     new = centre + c(at, 1) * lap + vertical
                 else:
-                    new = c(at, 0) * centre + c(at, 1) * sides_of(centre) + vertical
+                    new = c(at, 0) * centre + c(at, 1) * (sides_of(centre, pair) if level == 2 else rolled(centre)) + vertical
                 keep(level, at, new)
                 if level == STEPS:
                     o_ref[at, here, :] = new.astype(BF)
                 else:
                     levels[level][at] = new
                 del prev[at - 1]
-        return carry
-
-    lax.fori_loop(0, members // block, step, 0)
-
-
-def edge_body(f_ref, k_ref, ra_ref, rb_ref, d_ref, a_ref, o_ref, halo, dd, aa, new_rows, sems):
-    del f_ref
+
+    count = members // block
+    stage(0, 0)
+    for b in range(count):
+        if b + 1 < count:
+            stage(b + 1, (b + 1) % 2)
+        advance(b, b % 2)
+
+
+def edge_body(f_ref, picks_ref, info_ref, prec_ref, k_ref, ra_ref, rb_ref, d_ref, a_ref, *rest):
+    del f_ref, picks_ref, info_ref, prec_ref
+    o_ref, halo, dd, aa, new_rows, sems = rest
     members = k_ref.shape[1]
     lines = d_ref.shape[0]
     reach = STEPS * members
@@ -182,6 +207,7 @@
     dd[2 : 2 + lines, :] = d_ref[...]
     aa[2 : 2 + lines, :] = a_ref[...]
     across = laplace()
+    pair = beside()
     copies = []
     for side in range(2):
 
@@ -224,7 +250,8 @@
                     )
                     new = centre + dif * lap + vertical
                 else:
-                    new = (1.0 - 4.0 * dif) * centre + dif * sides_of(centre) + vertical
+                    around = sides_of(centre, pair) if level == 2 else rolled(centre)
+                    new = (1.0 - 4.0 * dif) * centre + dif * around + vertical
                 if level == STEPS:
                     slot = STEPS - 1 - away if side else away
                     new_rows[side * STEPS + slot] = new.astype(BF)
@@ -242,13 +269,27 @@
         copy.wait()
 
 
-def observe_body(s_ref, cell_ref, value_ref, rinv_ref, count_ref, loc_ref, h_ref, prec_ref):
+def prepare_body(cell_ref, value_ref, rinv_ref, count_ref, loc_ref, picks_ref, info_ref, prec_ref):
+    cells, slots = picks_ref.shape
+    cell = cell_ref[0]
+    line = lax.broadcasted_iota(jnp.int32, (cells, slots), 0)
+    picks_ref[...] = jnp.where(line == cell, 1.0, 0.0).astype(BF)
+    slot = lax.broadcasted_iota(jnp.int32, (1, slots), 1)
+    own = jnp.where(slot < count_ref[0, 0], rinv_ref[0], 0.0)
+    radius = (loc_ref[0].astype(F32) + 1.0) / 4.0
+    far = own * jnp.exp(-(radius * radius))
+    row = lax.broadcasted_iota(jnp.int32, (16, slots), 0)
+    value = value_ref[0].astype(F32)
+    info_ref[...] = jnp.where(row == 0, value, jnp.where(row == 1, far, 0.0)).astype(BF)
+    prec_ref[...] = jnp.where(
+        lax.broadcasted_iota(jnp.int32, (8, slots), 0) == 0, own, value
+    )
+
+
+def observe_body(s_ref, picks_ref, info_ref, h_ref):
     groups, tile, per, _ = s_ref.shape
     members = groups * per
-    slots = cell_ref.shape[-1]
-    cell = cell_ref[0]
-    total = jnp.zeros((members, slots), F32)
-    line = lax.broadcasted_iota(jnp.int32, (2 * LANES, slots), 0)
+    total = jnp.zeros((members, picks_ref.shape[1]), F32)
     for pair in range(tile // 2):
         here = jnp.concatenate(
             [
@@ -257,20 +298,10 @@
             ],
             axis=1,
         )
-        picks = jnp.where(line + 2 * LANES * pair == cell, 1.0, 0.0).astype(BF)
+        picks = picks_ref[2 * LANES * pair : 2 * LANES * (pair + 1), :]
         total += jnp.dot(here, picks, preferred_element_type=F32)
     h_ref[0:members, :] = total.astype(BF)
-    slot = lax.broadcasted_iota(jnp.int32, (1, slots), 1)
-    own = jnp.where(slot < count_ref[0, 0], rinv_ref[0], 0.0)
-    radius = (loc_ref[0].astype(F32) + 1.0) / 4.0
-    far = own * jnp.exp(-(radius * radius))
-    row = lax.broadcasted_iota(jnp.int32, (16, slots), 0)
-    value = value_ref[0].astype(F32)
-    info = jnp.where(row == 0, value, jnp.where(row == 1, far, 0.0))
-    h_ref[members:, :] = info.astype(BF)
-    prec_ref[...] = jnp.where(
-        lax.broadcasted_iota(jnp.int32, (8, slots), 0) == 0, own, value
-    )
+    h_ref[members:, :] = info_ref[...]
 
 
 def weigh(obs, value, prec):
@@ -299,53 +330,103 @@
     force_ref[...] = jnp.broadcast_to(force, (members, LANES))
 
 
-def analyse_body(ra_ref, rb_ref, xb_ref, xbar_ref, sys_ref, force_ref, o_ref):
+def analyse_body(ra_ref, rb_ref, xb_ref, xbar_ref, sys_ref, force_ref, o_ref, *scratch):
+    near, base, base_b, wide, square_b, tail_b, root, push = scratch
     members = sys_ref.shape[0]
     groups, tile, per, _ = o_ref.shape
-    total = sys_ref[...]
-    force = force_ref[:, 0:1]
-    for ref in (ra_ref, rb_ref):
+    slots = ra_ref.shape[1]
+    block = 64
+    blocks = [slice(i, i + block) for i in range(0, members, block)]
+    halves = [slice(i, i + 2 * LANES) for i in range(0, members, 2 * LANES)]
+
+    def on_diagonal(rows, value, other):
+        first = rows.start // LANES * LANES
+        line = lax.broadcasted_iota(jnp.int32, (block, LANES), 0) + (rows.start - first)
+        same = line == lax.broadcasted_iota(jnp.int32, (block, LANES), 1)
+        mine = other[:, first : first + LANES] + jnp.where(same, value, 0.0)
+        parts = [other[:, :first], mine, other[:, first + LANES :]]
+        return jnp.concatenate([p for p in parts if p.shape[1]], axis=1)
+
+    def product(left, right, into):
+        for half in halves:
+            into[:, half] = jnp.dot(left[...], right[:, half], preferred_element_type=F32)
+
+    for k, ref in enumerate((ra_ref, rb_ref)):
+        mean = jnp.zeros((8, slots), F32)
+        for rows in blocks:
+            mean += jnp.sum(ref[rows, :].astype(F32).reshape(block // 8, 8, slots), axis=0)
+        mean = jnp.sum(mean, axis=0, keepdims=True) * (1.0 / members)
         info = ref[members:, :].astype(F32)
-        scaled, more = weigh(ref[0:members, :].astype(F32), info[0:1, :], info[1:2, :])
-        total += gram(scaled)
-        force += more
-    diagonal = lax.broadcasted_iota(jnp.int32, (members, members), 0) == lax.broadcasted_iota(
-        jnp.int32, (members, members), 1
-    )
-    total += jnp.where(diagonal, members - 1.0, 0.0)
-    inv = lax.rsqrt(jnp.sum(total * total))
-    base = total * inv
-    base_b = base.astype(BF)
-    square = jnp.dot(base_b, base_b, preferred_element_type=F32)
-    tail = (0.0625 * square - 0.5625 * base).astype(BF)
-    root = (
-        jnp.where(diagonal, 2.25, 0.0)
-        - 2.4375 * base
-        + 1.6875 * square
-        + jnp.dot(square.astype(BF), tail, preferred_element_type=F32)
-    )
-    first = jnp.sum(root * force, axis=0, keepdims=True)
-    second = jnp.sum(root * first, axis=1, keepdims=True) * inv
-    mean_row = jnp.sum(jnp.where(diagonal, second, 0.0), axis=0, keepdims=True)
-    weights = (jnp.sqrt((members - 1.0) * inv) * root + mean_row).astype(BF)
+        prec = info[1:2, :]
+        scale = jnp.sqrt(prec)
+        weight = prec * (info[0:1, :] - mean)
+        for rows in blocks:
+            perturb = ref[rows, :].astype(F32) - mean
+            near[rows, k * slots : (k + 1) * slots] = (perturb * scale).astype(BF)
+            force = jnp.sum(perturb * weight, axis=1, keepdims=True)
+            before = force_ref[rows, :] if k == 0 else push[rows, :]
+            push[rows, :] = before + jnp.broadcast_to(force, (block, LANES))
+    for half in halves:
+        wide[:, half] = lax.dot_general(
+            near[...], near[half, :], (((1,), (1,)), ((), ())), preferred_element_type=F32
+        )
+    norm = jnp.zeros((8, members), F32)
+    for rows in blocks:
+        part = on_diagonal(rows, members - 1.0, wide[rows, :] + sys_ref[rows, :])
+        base[rows, :] = part
+        base_b[rows, :] = part.astype(BF)
+        norm += jnp.sum((part * part).reshape(block // 8, 8, members), axis=0)
+    inv = lax.rsqrt(jnp.sum(norm))
+    product(base_b, base_b, wide)
+    inv2 = inv * inv
+    for rows in blocks:
+        part = base[rows, :] * inv
+        square = wide[rows, :] * inv2
+        square_b[rows, :] = square.astype(BF)
+        tail_b[rows, :] = (0.0625 * square - 0.5625 * part).astype(BF)
+        root[rows, :] = on_diagonal(rows, 2.25, 1.6875 * square - 2.4375 * part)
+    product(square_b, tail_b, wide)
+    first = jnp.zeros((8, members), F32)
+    for rows in blocks:
+        part = root[rows, :] + wide[rows, :]
+        root[rows, :] = part
+        first += jnp.sum((part * push[rows, 0:1]).reshape(block // 8, 8, members), axis=0)
+    first = jnp.sum(first, axis=0, keepdims=True) * inv
+    means = []
+    for start in range(0, members, LANES):
+        total = jnp.zeros((8, LANES), F32)
+        for rows in (slice(start, start + block), slice(start + block, start + LANES)):
+            second = jnp.sum(root[rows, :] * first, axis=1, keepdims=True)
+            line = lax.broadcasted_iota(jnp.int32, (block, LANES), 0) + (rows.start - start)
+            same = line == lax.broadcasted_iota(jnp.int32, (block, LANES), 1)
+            total += jnp.sum(jnp.where(same, second, 0.0).reshape(block // 8, 8, LANES), axis=0)
+        means.append(jnp.sum(total, axis=0, keepdims=True))
+    mean_row = jnp.concatenate(means, axis=1)
+    gain = jnp.sqrt((members - 1.0) * inv)
+    for rows in blocks:
+        base_b[rows, :] = (gain * root[rows, :] + mean_row).astype(BF)
     for pair in range(tile // 2):
         cols = slice(2 * pair * LANES, 2 * (pair + 1) * LANES)
         new = xbar_ref[0:1, cols] + jnp.dot(
-            weights, xb_ref[:, cols], preferred_element_type=F32
+            base_b[...], xb_ref[:, cols], preferred_element_type=F32
         )
         for half in range(2):
             part = new[:, half * LANES : (half + 1) * LANES].astype(BF)
             o_ref[:, 2 * pair + half] = part.reshape(groups, per, LANES)
 
 
-def place_body(r_ref, o_ref, out):
-    lines = r_ref.shape[0]
-    block = o_ref.shape[0]
-    here = pl.ds(pl.multiple_of(pl.program_id(0) * block, block), block)
-    for row in range(lines):
-        out[row // 8, pl.ds(row % 8, block, stride=8), :] = r_ref[row, here, :].astype(F32)
+def place_body(r_ref, o_ref, out, sems):
+    lines, members, _ = r_ref.shape
+    copies = []
     for q in range(lines // 8):
-        o_ref[:, 8 * q : 8 * q + 8, :] = out[q].reshape(block, 8, LANES)
+        flat = out.at[q].reshape(members * 8, LANES)
+        for row in range(8):
+            flat[pl.ds(row, members, stride=8), :] = r_ref[8 * q + row].astype(F32)
+        copy = pltpu.make_async_copy(out.at[q], o_ref.at[:, q], sems.at[q])
+        copy.start()
+        copies.append(copy)
+    for copy in copies:
+        copy.wait()
 
 
 def program(members, diffusivity, advection, obs_value, obs_rinv, obs_cell, obs_count, loc_index):
@@ -381,13 +462,20 @@
     )
     got_b = lax.ppermute(send_b, "reg", across)
     got_a = lax.ppermute(send_a, "reg", near)
+    picks, info, prec = call(
+        prepare_body,
+        [((tile * LANES, slots), BF), ((16, slots), BF), ((8, slots), F32)],
+        5,
+        specs=[VMEM, VMEM, VMEM, SMEM, VMEM],
+        moved=1 << 20,
+    )(obs_cell, obs_value, obs_rinv, obs_count, loc_index)
     inner, kept = call(
         interior_body,
         [((lines, per, LANES), BF), ((2 * len(KEEP), per, LANES), F32)],
         3,
         [
-            pltpu.VMEM((lines // 8, 16 * 8, LANES), F32),
-            pltpu.VMEM((lines // 8, 16 * 8, LANES), F32),
+            pltpu.VMEM((2, lines // 8, BLOCK * 8, LANES), F32),
+            pltpu.VMEM((2, lines // 8, BLOCK * 8, LANES), F32),
             pltpu.VMEM((lines, 32, LANES), F32),
         ],
         moved=12 << 20,
@@ -395,7 +483,7 @@
     ahead = pl.pallas_call(
         edge_body,
         out_shape=jax.ShapeDtypeStruct((lines, per, LANES), BF),
-        in_specs=[pl.BlockSpec(memory_space=pl.ANY)] + [VMEM] * 5,
+        in_specs=[pl.BlockSpec(memory_space=pl.ANY)] * 4 + [VMEM] * 5,
         out_specs=pl.BlockSpec(memory_space=pl.ANY),
         input_output_aliases={0: 0},
         scratch_shapes=[
@@ -408,16 +496,15 @@
         cost_estimate=pl.CostEstimate(flops=0, bytes_accessed=2 << 20, transcendentals=0),
         compiler_params=pltpu.CompilerParams(vmem_limit_bytes=40 << 20),
         name="edge",
-    )(inner, kept, got_a, got_b, diffusivity, advection)
+    )(inner, picks, info, prec, kept, got_a, got_b, diffusivity, advection)
     states = lax.all_to_all(ahead.reshape(groups, tile, per, LANES), "mem", 0, 0)
-    obs, prec = call(
+    (obs,) = call(
         observe_body,
-        [((total + 16, slots), BF), ((8, slots), F32)],
-        6,
-        specs=[VMEM, VMEM, VMEM, VMEM, SMEM, VMEM],
+        [((total + 16, slots), BF)],
+        3,
         flops=2 * total * tile * LANES * slots,
         moved=2 << 20,
-    )(states, obs_cell, obs_value, obs_rinv, obs_count, loc_index)
+    )(states, picks, info)
     nb = lax.ppermute(obs, "reg", across)
     na = lax.ppermute(obs, "reg", near)
     xb, xbar, system, force = call(
@@ -436,21 +523,33 @@
         analyse_body,
         [((groups, tile, per, LANES), BF)],
         6,
+        [
+            pltpu.VMEM((total, 2 * slots), BF),
+            pltpu.VMEM((total, total), F32),
+            pltpu.VMEM((total, total), BF),
+            pltpu.VMEM((total, total), F32),
+            pltpu.VMEM((total, total), BF),
+            pltpu.VMEM((total, total), BF),
+            pltpu.VMEM((total, total), F32),
+            pltpu.VMEM((total, LANES), F32),
+        ],
         flops=10 * total * total * total,
         moved=4 << 20,
     )(na, nb, xb, xbar, system, force)
     home = lax.all_to_all(back, "mem", 0, 0).reshape(lines, per, LANES)
-    block = 32
-    return pl.pallas_call(
+    placed = pl.pallas_call(
         place_body,
-        grid=(per // block,),
-        out_shape=jax.ShapeDtypeStruct((per, lines, LANES), F32),
+        out_shape=jax.ShapeDtypeStruct((per, lines // 8, 8, LANES), F32),
         in_specs=[VMEM],
-        out_specs=pl.BlockSpec((block, lines, LANES), lambda i: (i, 0, 0)),
-        scratch_shapes=[pltpu.VMEM((lines // 8, block * 8, LANES), F32)],
+        out_specs=HBM,
+        scratch_shapes=[
+            pltpu.VMEM((lines // 8, per, 8, LANES), F32),
+            pltpu.SemaphoreType.DMA((lines // 8,)),
+        ],
         compiler_params=pltpu.CompilerParams(vmem_limit_bytes=40 << 20),
         name="place",
     )(home)
+    return placed.reshape(per, lines, LANES)
 
 
 def solution(mesh):

time: 75.4 us -> 72.3 us (0.959)
  blocking collectives: 13.3 us -> 27.9 us
  waiting for transfers between devices: 12.1 us -> 3.3 us
  starting transfers between devices: 35.1 us -> 29.7 us
  Pallas kernels: 13.8 us -> 10.3 us
    all_to_all x0 -> x1, blocking collectives: none -> 14.1 us  [program(): lax.all_to_all(ahead.reshape(groups, tile, per, LANES), 'mem', 0, 0)]
    all_to_all x1 -> x0, waiting for transfers between devices: 8.78 us -> none  [program(): lax.all_to_all(ahead.reshape(groups, tile, per, LANES), 'mem', 0, 0)]
    all_to_all x1 -> x0, starting transfers between devices: 4.84 us -> none  [program(): lax.all_to_all(ahead.reshape(groups, tile, per, LANES), 'mem', 0, 0)]
    pallas_call x1, Pallas kernels: 5 us -> 2.48 us  [program(): call(interior_body, [((lines, per, LANES), BF), ((2 * len(KEEP), per, LAN...]
    pallas_call x3 -> x4, Pallas kernels: 5.19 us -> 4.32 us  [the longest x1 2.29 us: program(): call(analyse_body, [((groups, tile, per, LANES), BF)], 6, [pltpu.VMEM((to...]
  transfers between devices with their start and end apart: 5 -> 4, of which waited for: 2 -> 1; matrix products, arithmetic and copies ran while one was open for 0% -> 0% of each run, Pallas kernels for 8% -> 5%
where the time goes in v3:
time: 72.3 us; the launch traced here: 72 us
  starting transfers between devices  29.7 us (41%)
  blocking collectives  27.9 us (39%)
  Pallas kernels  10.3 us (14%)
  waiting for transfers between devices  3.3 us (5%)
  between operations  0.79 us (1%)
    ppermute x1, starting transfers between devices, program(): got_b = lax.ppermute(send_b, 'reg', across)  17.6 us
    all_to_all x1, blocking collectives, program(): lax.all_to_all(ahead.reshape(groups, tile, per, LANES), 'mem', 0, 0)  14.1 us
    all_to_all x1, blocking collectives, program(): home = lax.all_to_all(back, 'mem', 0, 0).reshape(lines, per, LANES)  13.8 us
    ppermute x1, starting transfers between devices, program(): nb = lax.ppermute(obs, 'reg', across)  8.3 us
    ppermute x1, waiting for transfers between devices, program(): nb = lax.ppermute(obs, 'reg', across)  3.29 us
    pallas_call x1, Pallas kernels, program(): call(interior_body, [((lines, per, LANES), BF), ((2 * len(KEEP), per, LAN...  2.48 us
    pallas_call x1, Pallas kernels, program(): call(analyse_body, [((groups, tile, per, LANES), BF)], 6, [pltpu.VMEM((to...  2.29 us
    ppermute x1, starting transfers between devices, program(): na = lax.ppermute(obs, 'reg', near)  1.92 us
  transfers between devices with their start and end apart: 4, of which 1 were waited for; matrix products, arithmetic and copies ran while one was open for 0% of the time, Pallas kernels for 5%

profile of v3, /device:TPU:2, one launch (start us, length us, event | category | flops | bytes accessed | tf_op | source)
XLA Modules:
  0.0 72.0 jit_solution(16957844546508118664)
XLA Ops:
  0.0 0.0 copy-start.1
  0.0 0.0 copy-start.2
  0.0 0.0 copy-start
  0.0 0.0 copy-start.3
  0.0 1.5 %shard_map.82 = (bf16[400,128]{1,0:T(8,128)(2,1)S(1)}, bf16[400,128]{1,0:T(8,128)(2,1)S(1)}, bf16[128,32,128]{2,1,0:T(8,128)(2,1)S(1)}, f32[32,128]{1,0:T(8,128)S(1)}, f32[32,128]{1,0:T(8,128)S(1)}) custom-call(bf16[128,32,128]{2,1,0:T(8,128)(2,1)} %x_ref.1, f32[32,128]{1,0:T(8,128)} %d_ref.1, f32[32,128]{1,0:T(8,128)} %a_ref.1), custom_call_target="tpu_custom_call" | custom-call | bytes 1048576 | tf_op jit(solution)/shard_map/pallas_call | solution.py:443
  1.5 1.9 %collective-permute-start = (bf16[400,128]{1,0:T(8,128)(2,1)S(1)}, bf16[400,128]{1,0:T(8,128)(2,1)S(1)}, u32[]{:S(2)}, u32[]{:S(2)}) collective-permute-start(bf16[400,128]{1,0:T(8,128)(2,1)S(1)} %get-tuple-element.27), channel_id=1, source_target_pairs={{0,1},{1,0},{2,3},{3,2},{4,5},{5,4},{6,7},{7,6},{8,9},{9,8},{10,11... | collective-permute-start | bytes 307208 | tf_op jit(solution)/shard_map/ppermute | solution.py:464
  3.5 17.6 %collective-permute-start.1 = (bf16[400,128]{1,0:T(8,128)(2,1)S(1)}, bf16[400,128]{1,0:T(8,128)(2,1)S(1)}, u32[]{:S(2)}, u32[]{:S(2)}) collective-permute-start(bf16[400,128]{1,0:T(8,128)(2,1)S(1)} %get-tuple-element.28), channel_id=1, source_target_pairs={{0,191},{1,2},{2,1},{3,4},{4,3},{5,6},{6,5},{7,8},{8,7},{9,10},{10... | collective-permute-start | bytes 307208 | tf_op jit(solution)/shard_map/ppermute | solution.py:463
  21.7 2.5 %shard_map.83 = (bf16[32,128,128]{2,1,0:T(8,128)(2,1)S(1)}, f32[14,128,128]{2,1,0:T(8,128)S(1)}) custom-call(bf16[128,32,128]{2,1,0:T(8,128)(2,1)S(1)} %get-tuple-element.19.x_ref, f32[32,128]{1,0:T(8,128)S(1)} %get-tuple-element.20.d_ref, f32[32,128]{1,0:T(8,128)S(1)} %get-tuple-element.21.a_ref), custom_call_target="tpu_custom_call" | custom-call | bytes 12582912 | tf_op jit(solution)/shard_map/pallas_call | solution.py:472
  24.2 0.0 copy-done.1
  24.2 0.0 copy-done.2
  24.2 0.0 copy-done
  24.2 0.0 copy-done.3
  24.2 0.1 shard_map.84
  24.4 0.0 collective-permute-done.ra_ref
  24.4 0.0 collective-permute-done.1.rb_ref
  24.4 1.2 %edge.1 = bf16[32,128,128]{2,1,0:T(8,128)(2,1)S(1)} custom-call(bf16[32,128,128]{2,1,0:T(8,128)(2,1)S(1)} %get-tuple-element.22.f_ref, bf16[1024,256]{1,0:T(8,128)(2,1)S(1)} %get-tuple-element.23.picks_ref, bf16[16,256]{1,0:T(8,128)(2,1)S(1)} %get-tuple-element.24.info_ref, f32[8,256]{1,0:T(8,128)S(1)} %get-tuple-element.25.prec_ref, ...), custom_call_target="tpu_custom_call", output_to_operand_aliasing={{}: (0, {})} | custom-call | bytes 2097152 | tf_op jit(solution)/shard_map/edge/pallas_call | solution.py:483
  25.6 14.1 %all_to_all.10.s_ref = bf16[4,8,128,128]{3,2,1,0:T(8,128)(2,1)S(1)} all-to-all(bf16[4,8,128,128]{3,2,1,0:T(8,128)(2,1)S(1)} %bitcast.4), channel_id=1, replica_groups=mesh['mem'=4,'reg'=192] {'mem'}, dimensions={0} | all-to-all | bytes 2097152 | tf_op jit(solution)/shard_map/all_to_all | solution.py:500
  39.6 0.4 shard_map.85.h_ref
  40.1 1.9 %collective-permute-start.2 = (bf16[528,256]{1,0:T(8,128)(2,1)S(1)}, bf16[528,256]{1,0:T(8,128)(2,1)S(1)}, u32[]{:S(2)}, u32[]{:S(2)}) collective-permute-start(bf16[528,256]{1,0:T(8,128)(2,1)S(1)} %shard_map.85.h_ref), channel_id=1, source_target_pairs={{0,1},{1,0},{2,3},{3,2},{4,5},{5,4},{6,7},{7,6},{8,9},{9,8},{10,11... | collective-permute-start | bytes 811016 | tf_op jit(solution)/shard_map/ppermute | solution.py:509
  42.0 8.3 %collective-permute-start.3 = (bf16[528,256]{1,0:T(8,128)(2,1)S(1)}, bf16[528,256]{1,0:T(8,128)(2,1)S(1)}, u32[]{:S(2)}, u32[]{:S(2)}) collective-permute-start(bf16[528,256]{1,0:T(8,128)(2,1)S(1)} %shard_map.85.h_ref), channel_id=1, source_target_pairs={{0,191},{1,2},{2,1},{3,4},{4,3},{5,6},{6,5},{7,8},{8,7},{9,10},{10... | collective-permute-start | bytes 811016 | tf_op jit(solution)/shard_map/ppermute | solution.py:508
  50.3 0.8 %shard_map.86 = (bf16[512,1024]{1,0:T(8,128)(2,1)S(1)}, f32[8,1024]{1,0:T(8,128)S(1)}, f32[512,512]{1,0:T(8,128)S(1)}, f32[512,128]{1,0:T(8,128)S(1)}) custom-call(bf16[4,8,128,128]{3,2,1,0:T(8,128)(2,1)S(1)} %all_to_all.10.s_ref, bf16[528,256]{1,0:T(8,128)(2,1)S(1)} %shard_map.85.h_ref, f32[8,256]{1,0:T(8,128)S(1)} %get-tuple-element.25.prec_ref), custom_call_target="tpu_custom_call" | custom-call | flops 134217728 | bytes 4194304 | tf_op jit(solution)/shard_map/pallas_call | solution.py:510
  51.1 0.0 collective-permute-done.2.ra_ref
  51.1 3.3 %collective-permute-done.3.rb_ref = bf16[528,256]{1,0:T(8,128)(2,1)S(1)} collective-permute-done((bf16[528,256]{1,0:T(8,128)(2,1)S(1)}, bf16[528,256]{1,0:T(8,128)(2,1)S(1)}, u32[]{:S(2)}, u32[]{:S(2)}) %collective-permute-start.3) | collective-permute-done | bytes 270368 | tf_op jit(solution)/shard_map/ppermute | solution.py:508
  54.4 2.3 %shard_map.87 = bf16[4,8,128,128]{3,2,1,0:T(8,128)(2,1)S(1)} custom-call(bf16[528,256]{1,0:T(8,128)(2,1)S(1)} %collective-permute-done.2.ra_ref, bf16[528,256]{1,0:T(8,128)(2,1)S(1)} %collective-permute-done.3.rb_ref, bf16[512,1024]{1,0:T(8,128)(2,1)S(1)} %get-tuple-element.29.xb_ref, f32[8,1024]{1,0:T(8,128)S(1)} %get-tuple-element.30.xbar_ref, ...), custom_call_target="tpu_custom_call" | custom-call | flops 1342177280 | bytes 4194304 | tf_op jit(solution)/shard_map/pallas_call | solution.py:522
  56.7 13.8 %all_to_all.11 = bf16[4,8,128,128]{3,2,1,0:T(8,128)(2,1)S(1)} all-to-all(bf16[4,8,128,128]{3,2,1,0:T(8,128)(2,1)S(1)} %shard_map.87), channel_id=1, replica_groups=mesh['mem'=4,'reg'=192] {'mem'}, dimensions={0} | all-to-all | bytes 2097152 | tf_op jit(solution)/shard_map/all_to_all | solution.py:539
  70.5 1.5 %place.1 = f32[128,4,8,128]{3,2,1,0:T(8,128)} custom-call(bf16[32,128,128]{2,1,0:T(8,128)(2,1)S(1)} %bitcast.3), custom_call_target="tpu_custom_call" | custom-call | tf_op jit(solution)/shard_map/place/pallas_call | solution.py:540
Async XLA Ops:
  0.0 24.2 %copy-start.1 = (bf16[1,1,256]{2,1,0:T(2,128)(2,1)S(1)}, bf16[1,1,256]{2,1,0:T(2,128)(2,1)}, u32[]{:S(2)}) copy-start(bf16[1,1,256]{2,1,0:T(2,128)(2,1)} %value_ref.1) | copy-start | bytes 1540
  0.0 24.2 %copy-start.2 = (f32[1,1,256]{2,1,0:T(1,128)S(1)}, f32[1,1,256]{2,1,0:T(1,128)}, u32[]{:S(2)}) copy-start(f32[1,1,256]{2,1,0:T(1,128)} %rinv_ref.1) | copy-start | bytes 3076
  0.0 24.2 %copy-start = (s32[1,1,256]{2,1,0:T(1,128)S(1)}, s32[1,1,256]{2,1,0:T(1,128)}, u32[]{:S(2)}) copy-start(s32[1,1,256]{2,1,0:T(1,128)} %cell_ref.1) | copy-start | bytes 3076
  0.0 24.2 %copy-start.3 = (s32[1,1,256]{2,1,0:T(1,128)S(1)}, s32[1,1,256]{2,1,0:T(1,128)}, u32[]{:S(2)}) copy-start(s32[1,1,256]{2,1,0:T(1,128)} %loc_ref.1) | copy-start | bytes 3076
  1.5 22.8 %collective-permute-start = (bf16[400,128]{1,0:T(8,128)(2,1)S(1)}, bf16[400,128]{1,0:T(8,128)(2,1)S(1)}, u32[]{:S(2)}, u32[]{:S(2)}) collective-permute-start(bf16[400,128]{1,0:T(8,128)(2,1)S(1)} %get-tuple-element.27), channel_id=1, source_target_pairs={{0,1},{1,0},{2,3},{3,2},{4,5},{5,4},{6,7},{7,6},{8,9},{9,8},{10,11... | collective-permute-start | bytes 307208 | tf_op jit(solution)/shard_map/ppermute | solution.py:464
  3.5 20.9 %collective-permute-start.1 = (bf16[400,128]{1,0:T(8,128)(2,1)S(1)}, bf16[400,128]{1,0:T(8,128)(2,1)S(1)}, u32[]{:S(2)}, u32[]{:S(2)}) collective-permute-start(bf16[400,128]{1,0:T(8,128)(2,1)S(1)} %get-tuple-element.28), channel_id=1, source_target_pairs={{0,191},{1,2},{2,1},{3,4},{4,3},{5,6},{6,5},{7,8},{8,7},{9,10},{10... | collective-permute-start | bytes 307208 | tf_op jit(solution)/shard_map/ppermute | solution.py:463
  40.1 11.1 %collective-permute-start.2 = (bf16[528,256]{1,0:T(8,128)(2,1)S(1)}, bf16[528,256]{1,0:T(8,128)(2,1)S(1)}, u32[]{:S(2)}, u32[]{:S(2)}) collective-permute-start(bf16[528,256]{1,0:T(8,128)(2,1)S(1)} %shard_map.85.h_ref), channel_id=1, source_target_pairs={{0,1},{1,0},{2,3},{3,2},{4,5},{5,4},{6,7},{7,6},{8,9},{9,8},{10,11... | collective-permute-start | bytes 811016 | tf_op jit(solution)/shard_map/ppermute | solution.py:509
  42.0 12.4 %collective-permute-start.3 = (bf16[528,256]{1,0:T(8,128)(2,1)S(1)}, bf16[528,256]{1,0:T(8,128)(2,1)S(1)}, u32[]{:S(2)}, u32[]{:S(2)}) collective-permute-start(bf16[528,256]{1,0:T(8,128)(2,1)S(1)} %shard_map.85.h_ref), channel_id=1, source_target_pairs={{0,191},{1,2},{2,1},{3,4},{4,3},{5,6},{6,5},{7,8},{8,7},{9,10},{10... | collective-permute-start | bytes 811016 | tf_op jit(solution)/shard_map/ppermute | solution.py:508
